TPU v7x, 32 devices: a whole 2x2x4 slice. The times are simulated.
32 devices in a mesh: energy: 8 (over z, core), layer: 4 (over y, x).
Axes of the slice: x: 2, y: 2, z: 4, core: 2. Of those that a mesh axis runs over, the one named last changes fastest.
Arguments:
- green_blocks: bfloat16 [8, 12, 12, 1536], P('energy', None, None, 'layer'), as said below
- coupling: bfloat16 [12, 12, 4, 1536], P(None, None, None, 'layer'), may hold values from -1.75 to 1.75
- phonon_weights: float32 [2, 48, 4, 1536], P(None, None, None, 'layer'), may hold values from 0.001 to 0.01
- neighbours: int32 [4, 1536], P(None, 'layer'), may hold values from 0 to 1151, as said below
- phonon_shifts: int32 [48], replicated, may hold values from 1 to 2
Outputs:
- corrected: bfloat16 [8, 12, 12, 1536], P('energy', None, None, 'layer')
- polarization: float32 [48, 4, 1536], P(None, None, ('layer', 'energy'))
Inputs may be any that keep to these rules, and one draw needn't show every extreme that they name: Every 12 x 12 block green_blocks[E, :, :, a] is symmetric. neighbours[k, a] is a place in the window of atom a: places 0 to 383 are the previous layer block, then the own block, then the next one. Slot 0 lies in the previous block, slot 1 in the next block, the other slots in the own block and never name the atom itself.
All inputs are finite; a program needn't handle non-finite values.
Results may differ from a plain program's by a relative error of at most 0.0062.
Values may be sent and summed in bfloat16 or wider, within the bound.
A program may use at most 128 MiB of HBM per device.

v0:
```python
import functools
import math

import jax
import jax.numpy as jnp
import numpy as np
from jax import lax
from jax.experimental import pallas as pl
from jax.experimental.pallas import tpu as pltpu
from jax.sharding import PartitionSpec as P

MESH = pl.DeviceIdType.MESH
LANES = 128
F32 = jnp.float32
BF16 = jnp.bfloat16


def offsets(order):
    return [p * order - p * (p - 1) // 2 for p in range(order)]


def segments(order, packed):
    plan, start, first = [], 0, 0
    for i in range(0, order, 2):
        done = sum(order - n for n in range(i + 2))
        stop = packed if i + 2 >= order else done // 16 * 16
        if stop - start >= 32 or stop == packed:
            plan.append((start, stop, first, i + 2))
            start, first = stop, i + 2
    return plan


def expansion(order, row_stride, packed_rows):
    off = offsets(order)
    table = np.zeros((order * row_stride, packed_rows), np.float32)
    for p in range(order):
        for q in range(order):
            low, high = min(p, q), max(p, q)
            table[p * row_stride + q, off[low] + high - low] = 1.0
    return jnp.asarray(table, BF16)


def kernel(
    reach, shift_hbm, green_hbm, coup_hbm, weight_hbm, near_hbm, e12_hbm,
    e16_hbm, cor_ref, sum_ref,
    shift_ref, green_ref, coup_ref, weight_ref, near_ref, e12_ref, e16_ref, sig_ref,
    g16, s16, l16, tri32, own, halo, gin, pout, pin, pacc, hots, chunks, cin, c4, g3, pscr, ab,
    load_sem, hop_sem, halo_send, halo_recv, gin_send, gin_recv, part_send, part_recv,
    chunk_send, chunk_recv,
):
    order = green_ref.shape[0]
    atoms = green_ref.shape[2]
    nbr = near_ref.shape[0]
    freqs = shift_ref.shape[0]
    tiles = atoms // LANES
    packed = own.shape[0]
    pad = c4.shape[3]
    ne = lax.axis_size("energy")
    nl = lax.axis_size("layer")
    me = lax.axis_index("energy")
    layer = lax.axis_index("layer")
    share = atoms // ne
    off = offsets(order)
    plan = segments(order, packed)
    groups = (tuple(range(2, nbr)), (0, 1))

    def load(n, src, dst):
        copy = pltpu.make_async_copy(src, dst, load_sem.at[n])
        copy.start()
        return copy

    load_green = load(0, green_hbm, green_ref)
    load_near = load(1, near_hbm, near_ref)
    load_e12 = load(2, e12_hbm, e12_ref)
    load_coup = load(3, coup_hbm, coup_ref)
    load_weight = load(4, weight_hbm, weight_ref)
    load_shift = load(5, shift_hbm, shift_ref)
    load_e16 = load(6, e16_hbm, e16_ref)

    barrier = pltpu.get_barrier_semaphore()

    def greet(sem, energy, row):
        pl.semaphore_signal(
            sem, inc=1, device_id={"energy": energy, "layer": row}, device_id_type=MESH
        )

    def greet_near(sem):
        for d in range(1, reach + 1):

            @pl.when(me + d < ne)
            def _():
                greet(sem, me + d, layer)

            @pl.when(me >= d)
            def _():
                greet(sem, me - d, layer)

    near_count = jnp.minimum(me, reach) + jnp.minimum(ne - 1 - me, reach)
    rounds = -(-(ne - 1) // reach) - 1
    passed = []

    def pass_on():
        n = len(passed)
        if n < rounds:
            pl.semaphore_wait(hop_sem.at[n], near_count)
            if n + 1 < rounds:
                greet_near(hop_sem.at[n + 1])
            passed.append(n)

    greet_near(barrier)

    @pl.when(layer > 0)
    def _():
        pl.semaphore_signal(
            barrier, inc=1, device_id={"energy": me, "layer": layer - 1}, device_id_type=MESH
        )

    @pl.when(layer < nl - 1)
    def _():
        pl.semaphore_signal(
            barrier, inc=1, device_id={"energy": me, "layer": layer + 1}, device_id_type=MESH
        )

    tri32[...] = jnp.zeros_like(tri32)
    load_green.wait()
    for p in range(order):
        tri32[off[p] : off[p] + order - p, :] = green_ref[p].astype(F32)[p:, :]
    own[...] = tri32[...].astype(BF16)

    @pl.when(layer == 0)
    def _():
        halo[0] = jnp.zeros((packed, atoms), BF16)

    @pl.when(layer == nl - 1)
    def _():
        halo[1] = jnp.zeros((packed, atoms), BF16)

    for d in range(1, reach + 1):

        @pl.when(me < d)
        def _():
            gin[d - 1] = jnp.zeros((packed, atoms), BF16)
            pin[2 * d - 2] = jnp.zeros(pin.shape[1:], BF16)

        @pl.when(me + d >= ne)
        def _():
            pin[2 * d - 1] = jnp.zeros(pin.shape[1:], BF16)

    pl.semaphore_wait(
        barrier, near_count + (layer > 0).astype(jnp.int32) + (layer < nl - 1).astype(jnp.int32)
    )

    def remote(src, dst, send, recv, energy, row):
        return pltpu.make_async_remote_copy(
            src_ref=src, dst_ref=dst, send_sem=send, recv_sem=recv,
            device_id={"energy": energy, "layer": row}, device_id_type=MESH,
        )

    def halo_copy(side):
        row = layer + 1 if side == 0 else layer - 1
        return remote(own, halo.at[side], halo_send.at[side], halo_recv.at[side], me, row)

    def green_copy(d):
        return remote(
            own, gin.at[d - 1], gin_send.at[d - 1], gin_recv.at[d - 1], me + d, layer
        )

    def part_copy(slot, n, energy):
        start, stop, _, _ = plan[n]
        rows = pl.ds(start, stop - start)
        return remote(
            pout.at[slot, rows], pin.at[slot, rows], part_send.at[slot, n],
            part_recv.at[slot, n], energy, layer,
        )

    def chunk_copy(r):
        dest = lax.rem(me + r, ne)
        return remote(
            chunks.at[dest], cin.at[r], chunk_send.at[r], chunk_recv.at[r], dest, layer
        )

    has_above, has_below = layer < nl - 1, layer > 0

    @pl.when(has_above)
    def _():
        halo_copy(0).start()

    @pl.when(has_below)
    def _():
        halo_copy(1).start()

    for d in range(1, reach + 1):

        @pl.when(me + d < ne)
        def _():
            green_copy(d).start()

    if rounds:
        greet_near(hop_sem.at[0])

    row = lax.broadcasted_iota(jnp.int32, (atoms, atoms), 0)

    def one_hot(k, start):
        return jnp.where(row == near_ref[k : k + 1, :] - start, 1.0, 0.0).astype(BF16)

    def pick_neighbours(g, j, full, hot):
        size = len(groups[g])
        found = jnp.dot(full, hot, preferred_element_type=F32)
        for t in range(tiles):
            g3[pl.ds(t * size + j, order * order, stride=pad), :] = found[
                :, t * LANES : (t + 1) * LANES
            ]

    def expanded(block):
        return jnp.dot(e12_ref[...], block, preferred_element_type=F32).astype(BF16)

    load_near.wait()
    load_e12.wait()
    own_full = expanded(own[...])
    for j in range(len(groups[0])):
        pick_neighbours(0, j, own_full, one_hot(groups[0][j], atoms))
    hots[0] = one_hot(0, 0)
    hots[1] = one_hot(1, 2 * atoms)

    load_coup.wait()
    for g, slots in enumerate(groups):
        size = len(slots)
        for t in range(tiles):
            block = coup_ref[:, :, t * LANES : (t + 1) * LANES].astype(F32)
            block = block.reshape(order, order, nbr, LANES)
            c4[g, :, :, t * size : (t + 1) * size, :] = block[
                :, :, slots[0] : slots[0] + size, :
            ]

    last = off[-1] + 1
    for g in range(2):
        pscr[g, last * pad :, :] = jnp.zeros(((packed - last) * pad, LANES), F32)

    def products(g, start, stop):
        for i in range(start, stop, 2):
            first = jnp.zeros((2, order, pad, LANES), F32)
            for p in range(order):
                block = g3[p * order * pad : (p + 1) * order * pad, :]
                block = block.reshape(order, pad, LANES)
                first = first + c4[g, i : i + 2, p][:, None] * block[None]
            total = first[:, 0][:, None] * c4[g, i:, 0][None]
            for q in range(1, order):
                total = total + first[:, q][:, None] * c4[g, i:, q][None]
            total = total.astype(BF16).astype(F32)
            for n in range(2):
                pscr[g, off[i + n] * pad : (off[i + n] + order - i - n) * pad, :] = total[
                    n, n:
                ].reshape(-1, LANES)

    products(0, 0, order)

    load_weight.wait()
    load_shift.wait()

    def add_weights(w, sums):
        shift = shift_ref[w]
        low, high = weight_ref[w], weight_ref[freqs + w]
        new = []
        for d in range(1, reach + 1):
            pick = jnp.where(shift == d, 1.0, 0.0).astype(F32)
            new += [sums[2 * d - 2] + pick * low, sums[2 * d - 1] + pick * high]
        return tuple(new)

    sums = lax.fori_loop(
        0, freqs, add_weights, tuple(jnp.zeros((nbr, atoms), F32) for _ in range(2 * reach)),
        unroll=4,
    )
    for s in range(2 * reach):
        ab[s] = sums[s]

    def rows_of(g, t, j, start, stop):
        at = start * pad + t * len(groups[g]) + j
        return pscr[g, pl.ds(at, stop - start, stride=pad), :]

    def partials(g, t, s, start, stop):
        lanes = slice(t * LANES, (t + 1) * LANES)
        total = None
        for j, k in enumerate(groups[g]):
            term = ab[s, k : k + 1, lanes] * rows_of(g, t, j, start, stop)
            total = term if total is None else total + term
        return total

    for t in range(tiles):
        for s in range(2 * reach):
            pacc[s, :, t * LANES : (t + 1) * LANES] = partials(0, t, s, 0, packed)

    for d in range(1, reach + 1):

        @pl.when(me >= d)
        def _():
            green_copy(d).wait_recv()

    index = lax.broadcasted_iota(jnp.int32, (packed, LANES), 0)
    twice = jnp.full((packed, LANES), 2.0, F32)
    for p in range(order):
        twice = jnp.where(index == off[p], 1.0, twice)
    rows = [[None] * tiles for _ in range(reach * nbr)]

    def correlate(g, start, stop):
        for t in range(tiles):
            lanes = slice(t * LANES, (t + 1) * LANES)
            greens = [
                gin[d, start:stop, lanes].astype(F32) * twice[start:stop] for d in range(reach)
            ]
            for j, k in enumerate(groups[g]):
                value = rows_of(g, t, j, start, stop)
                for d in range(reach):
                    term = jnp.sum(greens[d] * value, axis=0, keepdims=True)
                    old = rows[d * nbr + k][t]
                    rows[d * nbr + k][t] = term if old is None else old + term

    correlate(0, 0, packed)

    pass_on()
    load_e16.wait()
    g16[...] = jnp.zeros_like(g16)
    for p in range(order):
        g16[p, :order, :] = green_ref[p].astype(F32)

    @pl.when(has_below)
    def _():
        halo_copy(0).wait_recv()

    @pl.when(has_above)
    def _():
        halo_copy(1).wait_recv()

    pick_neighbours(1, 0, expanded(halo[0]), hots[0])
    pick_neighbours(1, 1, expanded(halo[1]), hots[1])
    width = chunks.shape[2]

    for n, (start, stop, first, final) in enumerate(plan):
        products(1, first, final)
        if n == 0:
            pass_on()
        correlate(1, start, stop)
        if stop == packed:
            while len(passed) < rounds:
                pass_on()
            corr = jnp.concatenate([jnp.concatenate(r, axis=1) for r in rows], axis=0)
            for e in range(ne):
                moved = corr if e == 0 else pltpu.roll(corr, atoms - e * share, 1)
                chunks[e] = moved[:, :width]
            for r in range(1, ne):
                chunk_copy(r).start()
        for t in range(tiles):
            lanes = slice(t * LANES, (t + 1) * LANES)
            for s in range(2 * reach):
                total = pacc[s, start:stop, lanes] + partials(1, t, s, start, stop)
                pout[s, start:stop, lanes] = total.astype(BF16)
        for d in range(1, reach + 1):

            @pl.when(me + d < ne)
            def _():
                part_copy(2 * d - 2, n, me + d).start()

            @pl.when(me >= d)
            def _():
                part_copy(2 * d - 1, n, me - d).start()

    for n, (start, stop, _, _) in enumerate(plan):
        for d in range(1, reach + 1):

            @pl.when(me >= d)
            def _():
                part_copy(2 * d - 2, n, me).wait_recv()

            @pl.when(me + d < ne)
            def _():
                part_copy(2 * d - 1, n, me).wait_recv()

        sigma = pin[0, start:stop].astype(F32)
        for s in range(1, 2 * reach):
            sigma = sigma + pin[s, start:stop].astype(F32)
        sig_ref[start:stop, :] = sigma.astype(BF16)

    s16[...] = jnp.dot(
        e16_ref[...], sig_ref[...], preferred_element_type=F32
    ).reshape(s16.shape)

    for i in range(0, order, 2):
        left = [g16[i + n, 0:1, :] * s16[0] for n in range(2)]
        for p in range(1, order):
            block = s16[p]
            left = [left[n] + g16[i + n, p : p + 1, :] * block for n in range(2)]
        for n in range(2):
            l16[i + n] = left[n].astype(BF16).astype(F32)
    for i in range(0, order, 2):
        total = [g16[i + n] for n in range(2)]
        for p in range(order):
            block = g16[p]
            total = [total[n] + l16[i + n, p : p + 1, :] * block for n in range(2)]
        for n in range(2):
            cor_ref[i + n] = total[n][:order].astype(BF16)

    for r in range(1, ne):
        chunk_copy(r).wait_recv()
    summed = chunks[me]
    for r in range(1, ne):
        summed = summed + cin[r]
    sum_ref[...] = summed * (1.0 / (order * math.sqrt(ne)))

    @pl.when(has_above)
    def _():
        halo_copy(0).wait_send()

    @pl.when(has_below)
    def _():
        halo_copy(1).wait_send()

    for d in range(1, reach + 1):

        @pl.when(me + d < ne)
        def _():
            green_copy(d).wait_send()
            for n in range(len(plan)):
                part_copy(2 * d - 2, n, me).wait_send()

        @pl.when(me >= d)
        def _():
            for n in range(len(plan)):
                part_copy(2 * d - 1, n, me).wait_send()

    for r in range(1, ne):
        chunk_copy(r).wait_send()


def finish(reach, shift_ref, cor_ref, sum_ref, out_ref, pol_ref):
    nbr, share = pol_ref.shape[1:]
    freqs = shift_ref.shape[0]
    out_ref[...] = cor_ref[...]
    summed = sum_ref[:, :share]
    for w in range(freqs):
        shift = shift_ref[w]
        value = jnp.zeros((nbr, share), F32)
        for d in range(1, reach + 1):
            value = jnp.where(shift == d, summed[(d - 1) * nbr : d * nbr], value)
        pol_ref[w] = value


def body(green_blocks, coupling, phonon_weights, neighbours, phonon_shifts):
    ne = lax.axis_size("energy")
    reach = max(ne // 4, 1)
    order = green_blocks.shape[1]
    atoms = green_blocks.shape[3]
    nbr = neighbours.shape[0]
    freqs = phonon_shifts.shape[0]
    tiles = atoms // LANES
    share = atoms // ne
    count = order * (order + 1) // 2
    packed = -(-count // 16) * 16
    pad = -(-(tiles * max(nbr - 2, 2)) // 8) * 8
    rows = 16 * (-(-order // 16))
    width = -(-share // LANES) * LANES
    parts = len(segments(order, packed))
    vmem = pl.BlockSpec(memory_space=pltpu.VMEM)
    smem = pl.BlockSpec(memory_space=pltpu.SMEM)
    hbm = pl.BlockSpec(memory_space=pltpu.HBM)
    dma = pltpu.SemaphoreType.DMA
    green = green_blocks[0]
    result, summed = pl.pallas_call(
        functools.partial(kernel, reach),
        out_shape=(
            jax.ShapeDtypeStruct((order, order, atoms), BF16),
            jax.ShapeDtypeStruct((reach * nbr, width), F32),
        ),
        in_specs=[hbm] * 7,
        out_specs=(vmem, vmem),
        scratch_shapes=[
            pltpu.SMEM((freqs,), jnp.int32),
            pltpu.VMEM((order, order, atoms), BF16),
            pltpu.VMEM((order * order, nbr, atoms), BF16),
            pltpu.VMEM((2 * freqs, nbr, atoms), F32),
            pltpu.VMEM((nbr, atoms), jnp.int32),
            pltpu.VMEM((order * order, packed), BF16),
            pltpu.VMEM((order * rows, packed), BF16),
            pltpu.VMEM((packed, atoms), BF16),
            pltpu.VMEM((order, rows, atoms), F32),
            pltpu.VMEM((order, rows, atoms), F32),
            pltpu.VMEM((order, rows, atoms), F32),
            pltpu.VMEM((packed, atoms), F32),
            pltpu.VMEM((packed, atoms), BF16),
            pltpu.VMEM((2, packed, atoms), BF16),
            pltpu.VMEM((reach, packed, atoms), BF16),
            pltpu.VMEM((2 * reach, packed, atoms), BF16),
            pltpu.VMEM((2 * reach, packed, atoms), BF16),
            pltpu.VMEM((2 * reach, packed, atoms), F32),
            pltpu.VMEM((2, atoms, atoms), BF16),
            pltpu.VMEM((ne, reach * nbr, width), F32),
            pltpu.VMEM((ne, reach * nbr, width), F32),
            pltpu.VMEM((2, order, order, pad, LANES), F32),
            pltpu.VMEM((order * order * pad, LANES), F32),
            pltpu.VMEM((2, packed * pad, LANES), F32),
            pltpu.VMEM((2 * reach, nbr, atoms), F32),
            dma((7,)), pltpu.SemaphoreType.REGULAR((max(-(-(ne - 1) // reach) - 1, 1),)),
            dma((2,)), dma((2,)), dma((reach,)), dma((reach,)),
            dma((2 * reach, parts)), dma((2 * reach, parts)), dma((ne,)), dma((ne,)),
        ],
        compiler_params=pltpu.CompilerParams(
            collective_id=0, has_side_effects=True, vmem_limit_bytes=67043328
        ),
    )(
        phonon_shifts,
        green,
        coupling.reshape(order * order, nbr, atoms),
        phonon_weights.reshape(2 * freqs, nbr, atoms),
        neighbours,
        expansion(order, order, packed),
        expansion(order, rows, packed),
    )
    corrected, polarization = pl.pallas_call(
        functools.partial(finish, reach),
        out_shape=(
            jax.ShapeDtypeStruct((order, order, atoms), BF16),
            jax.ShapeDtypeStruct((freqs, nbr, share), F32),
        ),
        in_specs=[smem, vmem, vmem],
        out_specs=(vmem, vmem),
        compiler_params=pltpu.CompilerParams(vmem_limit_bytes=67043328),
    )(phonon_shifts, result, summed)
    return corrected[None], polarization


def solution(mesh):
    return jax.shard_map(
        body,
        mesh=mesh,
        in_specs=(
            P("energy", None, None, "layer"),
            P(None, None, None, "layer"),
            P(None, None, None, "layer"),
            P(None, "layer"),
            P(),
        ),
        out_specs=(P("energy", None, None, "layer"), P(None, None, ("layer", "energy"))),
        check_vma=False,
    )
```

profile of v0, /device:TPU:0, one launch (start us, length us, event | category | flops | bytes accessed | tf_op | source)
XLA Modules:
  0.0 18.7 jit_solution(15882360265853547462)
XLA Ops:
  0.6 16.3 %shard_map.86 = (bf16[12,12,384]{2,1,0:T(8,128)(2,1)}, f32[8,128]{1,0:T(8,128)}) custom-call(s32[48]{0:T(128)} %shift_ref.1, bf16[12,12,384]{2,1,0:T(8,128)(2,1)} %bitcast.6, bf16[144,4,384]{2,1,0:T(4,128)(2,1)} %bitcast.5, f32[96,4,384]{2,1,0:T(4,128)} %bitcast.4, s32[4,384]{1,0:T(4,128)} %near_hbm.1, bf16[144,80]{1,0:T(8,128)(2,1)} %constant.4.clone.e12_hbm, ...), custom_call_target="tpu_custom_call" | custom-call | tf_op jit(solution)/shard_map/pallas_call | solution.py:466
  17.0 1.7 %shard_map.87 = (bf16[12,12,384]{2,1,0:T(8,128)(2,1)}, f32[48,4,48]{2,1,0:T(4,128)}) custom-call(s32[48]{0:T(128)} %shift_ref.1, bf16[12,12,384]{2,1,0:T(8,128)(2,1)} %get-tuple-element.6.cor_ref, f32[8,128]{1,0:T(8,128)} %get-tuple-element.7.sum_ref), custom_call_target="tpu_custom_call" | custom-call | tf_op jit(solution)/shard_map/pallas_call | solution.py:516
where the time goes:
time: 18.8 us; the launch traced here: 18.7 us
  Pallas kernels  18 us (96%)
  between operations  0.64 us (3%)
    pallas_call x1, Pallas kernels, body(): pl.pallas_call(functools.partial(kernel, reach), out_shape=(jax.ShapeDtyp...  16.3 us
    pallas_call x1, Pallas kernels, body(): pl.pallas_call(functools.partial(finish, reach), out_shape=(jax.ShapeDtyp...  1.72 us

commit v1 on v0

--- a/solution.py
+++ b/solution.py
@@ -13,6 +13,7 @@
 LANES = 128
 F32 = jnp.float32
 BF16 = jnp.bfloat16
+VMEM_LIMIT = 48 * 1024 * 1024
 
 
 def offsets(order):
@@ -42,7 +43,7 @@
 
 def kernel(
     reach, shift_hbm, green_hbm, coup_hbm, weight_hbm, near_hbm, e12_hbm,
-    e16_hbm, cor_ref, sum_ref,
+    e16_hbm, cor_ref, pol_ref,
     shift_ref, green_ref, coup_ref, weight_ref, near_ref, e12_ref, e16_ref, sig_ref,
     g16, s16, l16, tri32, own, halo, gin, pout, pin, pacc, hots, chunks, cin, c4, g3, pscr, ab,
     load_sem, hop_sem, halo_send, halo_recv, gin_send, gin_recv, part_send, part_recv,
@@ -181,13 +182,13 @@
 
     has_above, has_below = layer < nl - 1, layer > 0
 
+    @pl.when(has_below)
+    def _():
+        halo_copy(1).start()
+
     @pl.when(has_above)
     def _():
         halo_copy(0).start()
-
-    @pl.when(has_below)
-    def _():
-        halo_copy(1).start()
 
     for d in range(1, reach + 1):
 
@@ -253,6 +254,7 @@
                 ].reshape(-1, LANES)
 
     products(0, 0, order)
+    pass_on()
 
     load_weight.wait()
     load_shift.wait()
@@ -288,6 +290,43 @@
     for t in range(tiles):
         for s in range(2 * reach):
             pacc[s, :, t * LANES : (t + 1) * LANES] = partials(0, t, s, 0, packed)
+
+    pass_on()
+    load_e16.wait()
+    g16[...] = jnp.zeros_like(g16)
+    for p in range(order):
+        g16[p, :order, :] = green_ref[p].astype(F32)
+    while len(passed) < rounds:
+        pass_on()
+
+    @pl.when(has_below)
+    def _():
+        halo_copy(0).wait_recv()
+
+    @pl.when(has_above)
+    def _():
+        halo_copy(1).wait_recv()
+
+    pick_neighbours(1, 0, expanded(halo[0]), hots[0])
+    pick_neighbours(1, 1, expanded(halo[1]), hots[1])
+    width = chunks.shape[2]
+
+    for n, (start, stop, first, final) in enumerate(plan):
+        products(1, first, final)
+        for t in range(tiles):
+            lanes = slice(t * LANES, (t + 1) * LANES)
+            for s in range(2 * reach):
+                total = pacc[s, start:stop, lanes] + partials(1, t, s, start, stop)
+                pout[s, start:stop, lanes] = total.astype(BF16)
+        for d in range(1, reach + 1):
+
+            @pl.when(me + d < ne)
+            def _():
+                part_copy(2 * d - 2, n, me + d).start()
+
+            @pl.when(me >= d)
+            def _():
+                part_copy(2 * d - 1, n, me - d).start()
 
     for d in range(1, reach + 1):
 
@@ -315,53 +354,13 @@
                     rows[d * nbr + k][t] = term if old is None else old + term
 
     correlate(0, 0, packed)
-
-    pass_on()
-    load_e16.wait()
-    g16[...] = jnp.zeros_like(g16)
-    for p in range(order):
-        g16[p, :order, :] = green_ref[p].astype(F32)
-
-    @pl.when(has_below)
-    def _():
-        halo_copy(0).wait_recv()
-
-    @pl.when(has_above)
-    def _():
-        halo_copy(1).wait_recv()
-
-    pick_neighbours(1, 0, expanded(halo[0]), hots[0])
-    pick_neighbours(1, 1, expanded(halo[1]), hots[1])
-    width = chunks.shape[2]
-
-    for n, (start, stop, first, final) in enumerate(plan):
-        products(1, first, final)
-        if n == 0:
-            pass_on()
-        correlate(1, start, stop)
-        if stop == packed:
-            while len(passed) < rounds:
-                pass_on()
-            corr = jnp.concatenate([jnp.concatenate(r, axis=1) for r in rows], axis=0)
-            for e in range(ne):
-                moved = corr if e == 0 else pltpu.roll(corr, atoms - e * share, 1)
-                chunks[e] = moved[:, :width]
-            for r in range(1, ne):
-                chunk_copy(r).start()
-        for t in range(tiles):
-            lanes = slice(t * LANES, (t + 1) * LANES)
-            for s in range(2 * reach):
-                total = pacc[s, start:stop, lanes] + partials(1, t, s, start, stop)
-                pout[s, start:stop, lanes] = total.astype(BF16)
-        for d in range(1, reach + 1):
-
-            @pl.when(me + d < ne)
-            def _():
-                part_copy(2 * d - 2, n, me + d).start()
-
-            @pl.when(me >= d)
-            def _():
-                part_copy(2 * d - 1, n, me - d).start()
+    correlate(1, 0, packed)
+    corr = jnp.concatenate([jnp.concatenate(r, axis=1) for r in rows], axis=0)
+    for e in range(ne):
+        moved = corr if e == 0 else pltpu.roll(corr, atoms - e * share, 1)
+        chunks[e] = moved[:, :width]
+    for r in range(1, ne):
+        chunk_copy(r).start()
 
     for n, (start, stop, _, _) in enumerate(plan):
         for d in range(1, reach + 1):
@@ -403,44 +402,46 @@
     summed = chunks[me]
     for r in range(1, ne):
         summed = summed + cin[r]
-    sum_ref[...] = summed * (1.0 / (order * math.sqrt(ne)))
-
-    @pl.when(has_above)
-    def _():
-        halo_copy(0).wait_send()
-
-    @pl.when(has_below)
-    def _():
-        halo_copy(1).wait_send()
-
-    for d in range(1, reach + 1):
-
-        @pl.when(me + d < ne)
-        def _():
-            green_copy(d).wait_send()
-            for n in range(len(plan)):
-                part_copy(2 * d - 2, n, me).wait_send()
-
-        @pl.when(me >= d)
-        def _():
-            for n in range(len(plan)):
-                part_copy(2 * d - 1, n, me).wait_send()
-
-    for r in range(1, ne):
-        chunk_copy(r).wait_send()
-
-
-def finish(reach, shift_ref, cor_ref, sum_ref, out_ref, pol_ref):
-    nbr, share = pol_ref.shape[1:]
-    freqs = shift_ref.shape[0]
-    out_ref[...] = cor_ref[...]
-    summed = sum_ref[:, :share]
+    summed = summed[:, :share] * (1.0 / (order * math.sqrt(ne)))
     for w in range(freqs):
         shift = shift_ref[w]
         value = jnp.zeros((nbr, share), F32)
         for d in range(1, reach + 1):
             value = jnp.where(shift == d, summed[(d - 1) * nbr : d * nbr], value)
         pol_ref[w] = value
+
+    @pl.when(has_above)
+    def _():
+        halo_copy(0).wait_send()
+
+    @pl.when(has_below)
+    def _():
+        halo_copy(1).wait_send()
+
+    for d in range(1, reach + 1):
+
+        @pl.when(me + d < ne)
+        def _():
+            green_copy(d).wait_send()
+            for n in range(len(plan)):
+                part_copy(2 * d - 2, n, me).wait_send()
+
+        @pl.when(me >= d)
+        def _():
+            for n in range(len(plan)):
+                part_copy(2 * d - 1, n, me).wait_send()
+
+    for r in range(1, ne):
+        chunk_copy(r).wait_send()
+
+
+def finish(cor_ref, pol_ref, cor_hbm, pol_hbm, sem):
+    first = pltpu.make_async_copy(cor_ref, cor_hbm, sem.at[0])
+    second = pltpu.make_async_copy(pol_ref, pol_hbm, sem.at[1])
+    first.start()
+    second.start()
+    first.wait()
+    second.wait()
 
 
 def body(green_blocks, coupling, phonon_weights, neighbours, phonon_shifts):
@@ -459,15 +460,14 @@
     width = -(-share // LANES) * LANES
     parts = len(segments(order, packed))
     vmem = pl.BlockSpec(memory_space=pltpu.VMEM)
-    smem = pl.BlockSpec(memory_space=pltpu.SMEM)
     hbm = pl.BlockSpec(memory_space=pltpu.HBM)
     dma = pltpu.SemaphoreType.DMA
     green = green_blocks[0]
-    result, summed = pl.pallas_call(
+    staged = pl.pallas_call(
         functools.partial(kernel, reach),
         out_shape=(
             jax.ShapeDtypeStruct((order, order, atoms), BF16),
-            jax.ShapeDtypeStruct((reach * nbr, width), F32),
+            jax.ShapeDtypeStruct((freqs, nbr, share), F32),
         ),
         in_specs=[hbm] * 7,
         out_specs=(vmem, vmem),
@@ -502,27 +502,33 @@
             dma((2 * reach, parts)), dma((2 * reach, parts)), dma((ne,)), dma((ne,)),
         ],
         compiler_params=pltpu.CompilerParams(
-            collective_id=0, has_side_effects=True, vmem_limit_bytes=67043328
+            collective_id=0, has_side_effects=True, vmem_limit_bytes=VMEM_LIMIT
         ),
     )(
-        phonon_shifts,
-        green,
-        coupling.reshape(order * order, nbr, atoms),
-        phonon_weights.reshape(2 * freqs, nbr, atoms),
-        neighbours,
-        expansion(order, order, packed),
-        expansion(order, rows, packed),
+        *(
+            pltpu.with_memory_space_constraint(x, pltpu.HBM)
+            for x in (
+                phonon_shifts,
+                green,
+                coupling.reshape(order * order, nbr, atoms),
+                phonon_weights.reshape(2 * freqs, nbr, atoms),
+                neighbours,
+                expansion(order, order, packed),
+                expansion(order, rows, packed),
+            )
+        )
     )
     corrected, polarization = pl.pallas_call(
-        functools.partial(finish, reach),
+        finish,
         out_shape=(
             jax.ShapeDtypeStruct((order, order, atoms), BF16),
             jax.ShapeDtypeStruct((freqs, nbr, share), F32),
         ),
-        in_specs=[smem, vmem, vmem],
-        out_specs=(vmem, vmem),
-        compiler_params=pltpu.CompilerParams(vmem_limit_bytes=67043328),
-    )(phonon_shifts, result, summed)
+        in_specs=[vmem, vmem],
+        out_specs=(hbm, hbm),
+        scratch_shapes=[dma((2,))],
+        compiler_params=pltpu.CompilerParams(vmem_limit_bytes=VMEM_LIMIT),
+    )(*staged)
     return corrected[None], polarization
 
 

time: 18.8 us -> 16.5 us (0.88)
  Pallas kernels: 18 us -> 15.7 us
    pallas_call x1, Pallas kernels: 16.3 us -> 15 us  [body(): pl.pallas_call(functools.partial(kernel, reach), out_shape=(jax.ShapeDtyp...]
    pallas_call x1, Pallas kernels: 1.72 us -> 0.71 us  [body(): pl.pallas_call(finish, out_shape=(jax.ShapeDtypeStruct((order, order, ato...]
where the time goes in v1:
time: 16.5 us; the launch traced here: 16.3 us
  Pallas kernels  15.7 us (95%)
  between operations  0.64 us (4%)
    pallas_call x1, Pallas kernels, body(): pl.pallas_call(functools.partial(kernel, reach), out_shape=(jax.ShapeDtyp...  15 us
    pallas_call x1, Pallas kernels, body(): pl.pallas_call(finish, out_shape=(jax.ShapeDtypeStruct((order, order, ato...  0.71 us

profile of v1, /device:TPU:0, one launch (start us, length us, event | category | flops | bytes accessed | tf_op | source)
XLA Modules:
  0.0 16.3 jit_solution(16493886648304252218)
XLA Ops:
  0.6 15.0 %shard_map.86 = (bf16[12,12,384]{2,1,0:T(8,128)(2,1)S(1)}, f32[48,4,48]{2,1,0:T(4,128)S(1)}) custom-call(s32[48]{0:T(128)} %shift_hbm.1, bf16[12,12,384]{2,1,0:T(8,128)(2,1)} %bitcast.6, bf16[144,4,384]{2,1,0:T(4,128)(2,1)} %bitcast.5, f32[96,4,384]{2,1,0:T(4,128)} %bitcast.4, s32[4,384]{1,0:T(4,128)} %near_hbm.1, bf16[144,80]{1,0:T(8,128)(2,1)} %constant.4.clone.e12_hbm, ...), custom_call_target="tpu_custom_call" | custom-call | tf_op jit(solution)/shard_map/pallas_call | solution.py:466
  15.6 0.7 %shard_map.87 = (bf16[12,12,384]{2,1,0:T(8,128)(2,1)}, f32[48,4,48]{2,1,0:T(4,128)}) custom-call(bf16[12,12,384]{2,1,0:T(8,128)(2,1)S(1)} %get-tuple-element.6.cor_ref, f32[48,4,48]{2,1,0:T(4,128)S(1)} %get-tuple-element.7.pol_ref), custom_call_target="tpu_custom_call" | custom-call | tf_op jit(solution)/shard_map/pallas_call | solution.py:521

commit v2 on v1

v2 whole, which is shorter than its diff:
```python
import functools
import math

import jax
import jax.numpy as jnp
from jax import lax
from jax.experimental import pallas as pl
from jax.experimental.pallas import tpu as pltpu
from jax.sharding import PartitionSpec as P

MESH = pl.DeviceIdType.MESH
LANES = 128
F32 = jnp.float32
BF16 = jnp.bfloat16
VMEM_LIMIT = 48 * 1024 * 1024


def offsets(order):
    return [p * order - p * (p - 1) // 2 for p in range(order)]


def segments(order, packed):
    off = offsets(order)
    plan, start, first = [], 0, 0
    for rows in (2, 4):
        if rows < order and off[rows] // 16 * 16 > start:
            stop = off[rows] // 16 * 16
            plan.append((start, stop, first, rows))
            start, first = stop, rows
    middle = start + (packed - start) * 2 // 3 // 16 * 16
    if middle > start:
        plan.append((start, middle, first, order))
        start, first = middle, order
    return plan + [(start, packed, first, order)]


def complete(order, stop):
    return sum(o + order - p <= stop for p, o in enumerate(offsets(order)))


def expansion(order, row_stride, packed_rows):
    row = lax.broadcasted_iota(jnp.int32, (order * row_stride, packed_rows), 0)
    column = lax.broadcasted_iota(jnp.int32, (order * row_stride, packed_rows), 1)
    p, q = row // row_stride, row % row_stride
    low, high = jnp.minimum(p, q), jnp.maximum(p, q)
    entry = low * order - low * (low - 1) // 2 + high - low
    return jnp.where((entry == column) & (q < order), 1.0, 0.0).astype(BF16)


def kernel(
    reach, shift_hbm, green_hbm, coup_hbm, weight_hbm, near_hbm, cor_ref, pol_ref,
    shift_ref, green_ref, coup_ref, weight_ref, near_ref, e16_ref, sig_ref,
    g16, s16, l16, tri32, own, halo, gin, pout, pin, pacc, hots, chunks, cin, c4, g3, g3b, pscr, ab,
    load_sem, side_sem, near_sem, far_sem, halo_send, halo_recv, gin_send, gin_recv, part_send, part_recv,
    chunk_send, chunk_recv,
):
    order = green_ref.shape[0]
    atoms = green_ref.shape[2]
    nbr = near_ref.shape[0]
    freqs = shift_ref.shape[0]
    tiles = atoms // LANES
    packed = own.shape[0]
    pad = c4.shape[3]
    ne = lax.axis_size("energy")
    nl = lax.axis_size("layer")
    me = lax.axis_index("energy")
    layer = lax.axis_index("layer")
    share = atoms // ne
    depth = s16.shape[1]
    off = offsets(order)
    plan = segments(order, packed)
    groups = (tuple(range(2, nbr)), (0, 1))

    def load(n, src, dst):
        copy = pltpu.make_async_copy(src, dst, load_sem.at[n])
        copy.start()
        return copy

    load_green = load(0, green_hbm, green_ref)
    load_near = load(1, near_hbm, near_ref)
    load_coup = load(2, coup_hbm, coup_ref)
    load_weight = load(3, weight_hbm, weight_ref)
    load_shift = load(4, shift_hbm, shift_ref)

    barrier = pltpu.get_barrier_semaphore()

    def greet(sem, energy, row):
        pl.semaphore_signal(
            sem, inc=1, device_id={"energy": energy, "layer": row}, device_id_type=MESH
        )

    odd = lax.rem(me, 2) == 1
    even = jnp.logical_not(odd)
    has_above, has_below = layer < nl - 1, layer > 0
    near_above = jnp.minimum(ne - 1 - me, reach)
    near_count = near_above + jnp.minimum(me, reach)
    far_above = ne - 1 - me - near_above

    for d in range(1, ne):

        @pl.when(me + d < ne)
        def _():
            greet(barrier, me + d, layer)

    @pl.when(has_above)
    def _():
        greet(barrier, me, layer + 1)

    @pl.when(has_below)
    def _():
        greet(barrier, me - lax.rem(me, 2) + 1, layer - 1)

    @pl.when(odd)
    def _():
        greet(barrier, me - 1, layer)

    tri32[...] = jnp.zeros_like(tri32)
    e16_ref[...] = expansion(order, depth, packed)
    load_green.wait()
    for p in range(order):
        tri32[off[p] : off[p] + order - p, :] = green_ref[p].astype(F32)[p:, :]
    own[...] = tri32[...].astype(BF16)

    @pl.when(jnp.logical_not(has_above & has_below))
    def _():
        g3b[...] = jnp.zeros_like(g3b)

    for d in range(1, reach + 1):

        @pl.when(me < d)
        def _():
            gin[d - 1] = jnp.zeros((packed, atoms), BF16)
            pin[2 * d - 2] = jnp.zeros(pin.shape[1:], BF16)

        @pl.when(me + d >= ne)
        def _():
            pin[2 * d - 1] = jnp.zeros(pin.shape[1:], BF16)

    pl.semaphore_wait(
        barrier,
        me
        + even.astype(jnp.int32)
        + has_below.astype(jnp.int32)
        + 2 * (odd & has_above).astype(jnp.int32),
    )

    def remote(src, dst, send, recv, energy, row):
        return pltpu.make_async_remote_copy(
            src_ref=src, dst_ref=dst, send_sem=send, recv_sem=recv,
            device_id={"energy": energy, "layer": row}, device_id_type=MESH,
        )

    def halo_copy(side):
        row = layer + 1 if side == 0 else layer - 1
        return remote(own, halo.at[side], halo_send.at[0], halo_recv.at[side], me, row)

    def green_copy(d):
        return remote(
            own, gin.at[d - 1], gin_send.at[0], gin_recv.at[0], me + d, layer
        )

    def part_copy(slot, n, energy):
        start, stop, _, _ = plan[n]
        rows = pl.ds(start, stop - start)
        return remote(
            pout.at[slot, rows], pin.at[slot, rows], part_send.at[0], part_recv.at[n],
            energy, layer,
        )

    def chunk_copy(r):
        dest = lax.rem(me + r, ne)
        return remote(
            chunks.at[dest], cin.at[r], chunk_send.at[0], chunk_recv.at[0], dest, layer
        )

    def wait_gin(send):
        number = jnp.minimum(ne - 1 - me, reach) if send else jnp.minimum(me, reach)
        for c in range(1, reach + 1):

            @pl.when(number == c)
            def _():
                some = gin.at[pl.ds(0, c)]
                copy = remote(some, some, gin_send.at[0], gin_recv.at[0], me, layer)
                copy.wait_send() if send else copy.wait_recv()

    def wait_parts(rows, recv, send):
        for c in range(1, 2 * reach + 1):

            @pl.when(near_count == c)
            def _():
                some = pin.at[pl.ds(0, c), rows]
                copy = remote(some, some, part_send.at[0], part_recv.at[recv], me, layer)
                copy.wait_send() if send else copy.wait_recv()

    def wait_chunks():
        some = cin.at[pl.ds(1, ne - 1)]
        return remote(some, some, chunk_send.at[0], chunk_recv.at[0], me, layer)

    @pl.when(has_below)
    def _():
        halo_copy(1).start()

    @pl.when(odd & has_above)
    def _():
        halo_copy(0).start()
        greet(side_sem, me - 1, layer)

    for d in range(1, ne):

        @pl.when(me >= d)
        def _():
            greet(near_sem if d <= reach else far_sem, me - d, layer)

    picked = (g3, g3b)
    row = lax.broadcasted_iota(jnp.int32, (atoms, atoms), 0)

    def one_hot(k, start):
        return jnp.where(row == near_ref[k : k + 1, :] - start, 1.0, 0.0).astype(BF16)

    def pick_neighbours(g, j, blocks, hot):
        size = len(groups[g])
        found = jnp.dot(blocks, hot, preferred_element_type=F32)
        for t in range(tiles):
            picked[g][pl.ds(t * size + j, packed, stride=pad), :] = found[
                :, t * LANES : (t + 1) * LANES
            ]

    load_near.wait()
    for j in range(len(groups[0])):
        pick_neighbours(0, j, own[...], one_hot(groups[0][j], atoms))
    hots[0] = one_hot(0, 0)
    hots[1] = one_hot(1, 2 * atoms)

    load_coup.wait()
    for g, slots in enumerate(groups):
        size = len(slots)
        for t in range(tiles):
            block = coup_ref[:, :, t * LANES : (t + 1) * LANES].astype(F32)
            block = block.reshape(order, order, nbr, LANES)
            c4[g, :, :, t * size : (t + 1) * size, :] = block[
                :, :, slots[0] : slots[0] + size, :
            ]

    last = off[-1] + 1
    for g in range(2):
        pscr[g, last * pad :, :] = jnp.zeros(((packed - last) * pad, LANES), F32)

    def entry(g, low, high):
        at = (off[low] + high - low) * pad
        return picked[g][at : at + pad, :]

    def products(g, start, stop):
        for i in range(start, stop, 2):
            first = jnp.zeros((2, order, pad, LANES), F32)
            for p in range(order):
                block = jnp.stack([entry(g, min(p, q), max(p, q)) for q in range(order)])
                first = first + c4[g, i : i + 2, p][:, None] * block[None]
            total = first[:, 0][:, None] * c4[g, i:, 0][None]
            for q in range(1, order):
                total = total + first[:, q][:, None] * c4[g, i:, q][None]
            total = total.astype(BF16).astype(F32)
            for n in range(2):
                pscr[g, off[i + n] * pad : (off[i + n] + order - i - n) * pad, :] = total[
                    n, n:
                ].reshape(-1, LANES)

    @pl.when(even & has_above)
    def _():
        pl.semaphore_wait(side_sem, 1)
        halo_copy(0).start()

    @pl.when(near_above > 0)
    def _():
        pl.semaphore_wait(near_sem, near_above)

    for d in range(1, reach + 1):

        @pl.when(me + d < ne)
        def _():
            green_copy(d).start()

    products(0, 0, order)

    load_weight.wait()
    load_shift.wait()

    def add_weights(w, sums):
        shift = shift_ref[w]
        low, high = weight_ref[w], weight_ref[freqs + w]
        new = []
        for d in range(1, reach + 1):
            pick = jnp.where(shift == d, 1.0, 0.0).astype(F32)
            new += [sums[2 * d - 2] + pick * low, sums[2 * d - 1] + pick * high]
        return tuple(new)

    sums = lax.fori_loop(
        0, freqs, add_weights, tuple(jnp.zeros((nbr, atoms), F32) for _ in range(2 * reach)),
        unroll=4,
    )
    for s in range(2 * reach):
        ab[s] = sums[s]

    def rows_of(g, t, j, start, stop):
        at = start * pad + t * len(groups[g]) + j
        return pscr[g, pl.ds(at, stop - start, stride=pad), :]

    def partials(g, t, s, start, stop):
        lanes = slice(t * LANES, (t + 1) * LANES)
        total = None
        for j, k in enumerate(groups[g]):
            term = ab[s, k : k + 1, lanes] * rows_of(g, t, j, start, stop)
            total = term if total is None else total + term
        return total

    for t in range(tiles):
        for s in range(2 * reach):
            pacc[s, :, t * LANES : (t + 1) * LANES] = partials(0, t, s, 0, packed)

    g16[...] = jnp.zeros_like(g16)
    for p in range(order):
        g16[p, :order, :] = green_ref[p].astype(F32)
    sig_ref[...] = jnp.zeros_like(sig_ref)

    @pl.when(has_above)
    def _():
        halo_copy(1).wait_recv()
        pick_neighbours(1, 1, halo[1], hots[1])

    @pl.when(has_below)
    def _():
        halo_copy(0).wait_recv()
        pick_neighbours(1, 0, halo[0], hots[0])


    send_order = [(1 - 2 * (d % 2 == 0)) * d for d in range(1, reach + 1)]
    send_order += [-d for d in send_order]

    def correlations():
        @pl.when(far_above > 0)
        def _():
            pl.semaphore_wait(far_sem, far_above)

        wait_gin(False)

        index = lax.broadcasted_iota(jnp.int32, (packed, LANES), 0)
        twice = jnp.full((packed, LANES), 2.0, F32)
        for p in range(order):
            twice = jnp.where(index == off[p], 1.0, twice)
        rows = [[None] * tiles for _ in range(reach * nbr)]

        def correlate(g, start, stop):
            for t in range(tiles):
                lanes = slice(t * LANES, (t + 1) * LANES)
                greens = [
                    gin[d, start:stop, lanes].astype(F32) * twice[start:stop] for d in range(reach)
                ]
                for j, k in enumerate(groups[g]):
                    value = rows_of(g, t, j, start, stop)
                    for d in range(reach):
                        term = jnp.sum(greens[d] * value, axis=0, keepdims=True)
                        old = rows[d * nbr + k][t]
                        rows[d * nbr + k][t] = term if old is None else old + term

        correlate(0, 0, packed)
        correlate(1, 0, packed)
        sums = [jnp.concatenate([r[t] for r in rows], axis=0) for t in range(tiles)]
        lane = lax.broadcasted_iota(jnp.int32, sums[0].shape, 1)
        for e in range(ne):
            start = e * share % LANES
            low, high = e * share // LANES, (e * share + share - 1) // LANES
            chunks[e] = sums[low] if low == high else jnp.where(lane >= start, sums[low], sums[high])
        for r in range(1, ne):
            chunk_copy(r).start()

    for n, (start, stop, first, final) in enumerate(plan):
        if first < final:
            products(1, first, final)
            if final == order:
                correlations()
        for t in range(tiles):
            lanes = slice(t * LANES, (t + 1) * LANES)
            for s in range(2 * reach):
                total = pacc[s, start:stop, lanes] + partials(1, t, s, start, stop)
                pout[s, start:stop, lanes] = total.astype(BF16)
        for d in send_order:
            if d > 0:

                @pl.when(me + d < ne)
                def _():
                    part_copy(2 * d - 2, n, me + d).start()
            else:

                @pl.when(me >= -d)
                def _():
                    part_copy(-2 * d - 1, n, me + d).start()

    for n, (start, stop, _, _) in enumerate(plan):
        first, final = complete(order, start), complete(order, stop)
        wait_parts(pl.ds(start, stop - start), n, False)
        sigma = pin[0, start:stop].astype(F32)
        for s in range(1, 2 * reach):
            sigma = sigma + pin[s, start:stop].astype(F32)
        sig_ref[start:stop, :] = sigma.astype(BF16)
        s16[first:final] = jnp.dot(
            e16_ref[first * depth : final * depth, :], sig_ref[...], preferred_element_type=F32
        ).reshape(final - first, depth, atoms)
        for i in range(0, order, 2):
            left = [None if first == 0 else l16[i + m] for m in range(2)]
            for p in range(first, final):
                block = s16[p]
                for m in range(2):
                    term = g16[i + m, p : p + 1, :] * block
                    left[m] = term if left[m] is None else left[m] + term
            for m in range(2):
                l16[i + m] = left[m].astype(BF16).astype(F32) if stop == packed else left[m]

    for i in range(0, order, 2):
        total = [g16[i + n] for n in range(2)]
        for p in range(order):
            block = g16[p]
            total = [total[n] + l16[i + n, p : p + 1, :] * block for n in range(2)]
        for n in range(2):
            cor_ref[i + n] = total[n][:order].astype(BF16)

    wait_chunks().wait_recv()
    summed = chunks[me]
    for r in range(1, ne):
        summed = summed + cin[r]
    summed = pltpu.roll(summed, lax.rem(ne * LANES - me * share, LANES), 1)
    summed = summed[:, :share] * (1.0 / (order * math.sqrt(ne)))
    for w in range(freqs):
        shift = shift_ref[w]
        value = jnp.zeros((nbr, share), F32)
        for d in range(1, reach + 1):
            value = jnp.where(shift == d, summed[(d - 1) * nbr : d * nbr], value)
        pol_ref[w] = value

    for c in range(1, 3):

        @pl.when(has_above.astype(jnp.int32) + has_below.astype(jnp.int32) == c)
        def _():
            some = halo.at[pl.ds(0, c)]
            remote(some, some, halo_send.at[0], halo_recv.at[0], me, layer).wait_send()

    wait_gin(True)
    wait_parts(pl.ds(0, packed), 0, True)
    wait_chunks().wait_send()


def finish(cor_ref, pol_ref, cor_hbm, pol_hbm, sem):
    first = pltpu.make_async_copy(cor_ref, cor_hbm, sem.at[0])
    second = pltpu.make_async_copy(pol_ref, pol_hbm, sem.at[1])
    first.start()
    second.start()
    first.wait()
    second.wait()


def body(green_blocks, coupling, phonon_weights, neighbours, phonon_shifts):
    ne = lax.axis_size("energy")
    reach = max(ne // 4, 1)
    order = green_blocks.shape[1]
    atoms = green_blocks.shape[3]
    nbr = neighbours.shape[0]
    freqs = phonon_shifts.shape[0]
    tiles = atoms // LANES
    share = atoms // ne
    count = order * (order + 1) // 2
    packed = -(-count // 16) * 16
    pad = -(-(tiles * max(nbr - 2, 2)) // 8) * 8
    rows = 16 * (-(-order // 16))
    parts = len(segments(order, packed))
    vmem = pl.BlockSpec(memory_space=pltpu.VMEM)
    hbm = pl.BlockSpec(memory_space=pltpu.HBM)
    dma = pltpu.SemaphoreType.DMA
    green = green_blocks[0]
    staged = pl.pallas_call(
        functools.partial(kernel, reach),
        out_shape=(
            jax.ShapeDtypeStruct((order, order, atoms), BF16),
            jax.ShapeDtypeStruct((freqs, nbr, share), F32),
        ),
        in_specs=[hbm] * 5,
        out_specs=(vmem, vmem),
        scratch_shapes=[
            pltpu.SMEM((freqs,), jnp.int32),
            pltpu.VMEM((order, order, atoms), BF16),
            pltpu.VMEM((order * order, nbr, atoms), BF16),
            pltpu.VMEM((2 * freqs, nbr, atoms), F32),
            pltpu.VMEM((nbr, atoms), jnp.int32),
            pltpu.VMEM((order * rows, packed), BF16),
            pltpu.VMEM((packed, atoms), BF16),
            pltpu.VMEM((order, rows, atoms), F32),
            pltpu.VMEM((order, rows, atoms), F32),
            pltpu.VMEM((order, rows, atoms), F32),
            pltpu.VMEM((packed, atoms), F32),
            pltpu.VMEM((packed, atoms), BF16),
            pltpu.VMEM((2, packed, atoms), BF16),
            pltpu.VMEM((reach, packed, atoms), BF16),
            pltpu.VMEM((2 * reach, packed, atoms), BF16),
            pltpu.VMEM((2 * reach, packed, atoms), BF16),
            pltpu.VMEM((2 * reach, packed, atoms), F32),
            pltpu.VMEM((2, atoms, atoms), BF16),
            pltpu.VMEM((ne, reach * nbr, LANES), F32),
            pltpu.VMEM((ne, reach * nbr, LANES), F32),
            pltpu.VMEM((2, order, order, pad, LANES), F32),
            pltpu.VMEM((packed * pad, LANES), F32),
            pltpu.VMEM((packed * pad, LANES), F32),
            pltpu.VMEM((2, packed * pad, LANES), F32),
            pltpu.VMEM((2 * reach, nbr, atoms), F32),
            dma((5,)), *[pltpu.SemaphoreType.REGULAR] * 3,
            dma((1,)), dma((2,)), dma((1,)), dma((1,)), dma((1,)), dma((parts,)), dma((1,)), dma((1,)),
        ],
        compiler_params=pltpu.CompilerParams(
            collective_id=0, has_side_effects=True, vmem_limit_bytes=VMEM_LIMIT
        ),
    )(
        *(
            pltpu.with_memory_space_constraint(x, pltpu.HBM)
            for x in (
                phonon_shifts,
                green,
                coupling.reshape(order * order, nbr, atoms),
                phonon_weights.reshape(2 * freqs, nbr, atoms),
                neighbours,
            )
        )
    )
    corrected, polarization = pl.pallas_call(
        finish,
        out_shape=(
            jax.ShapeDtypeStruct((order, order, atoms), BF16),
            jax.ShapeDtypeStruct((freqs, nbr, share), F32),
        ),
        in_specs=[vmem, vmem],
        out_specs=(hbm, hbm),
        scratch_shapes=[dma((2,))],
        compiler_params=pltpu.CompilerParams(vmem_limit_bytes=VMEM_LIMIT),
    )(*staged)
    return corrected[None], polarization


def solution(mesh):
    return jax.shard_map(
        body,
        mesh=mesh,
        in_specs=(
            P("energy", None, None, "layer"),
            P(None, None, None, "layer"),
            P(None, None, None, "layer"),
            P(None, "layer"),
            P(),
        ),
        out_specs=(P("energy", None, None, "layer"), P(None, None, ("layer", "energy"))),
        check_vma=False,
    )
```

time: 16.5 us -> 15.1 us (0.915)
  Pallas kernels: 15.7 us -> 14.3 us
    pallas_call x1, Pallas kernels: 15 us -> 13.6 us  [body(): pl.pallas_call(functools.partial(kernel, reach), out_shape=(jax.ShapeDtyp...]
where the time goes in v2:
time: 15.1 us; the launch traced here: 14.9 us
  Pallas kernels  14.3 us (95%)
  between operations  0.64 us (4%)
    pallas_call x1, Pallas kernels, body(): pl.pallas_call(functools.partial(kernel, reach), out_shape=(jax.ShapeDtyp...  13.6 us
    pallas_call x1, Pallas kernels, body(): pl.pallas_call(finish, out_shape=(jax.ShapeDtypeStruct((order, order, ato...  0.71 us

profile of v2, /device:TPU:0, one launch (start us, length us, event | category | flops | bytes accessed | tf_op | source)
XLA Modules:
  0.0 14.9 jit_solution(4359561919732138273)
XLA Ops:
  0.6 13.6 %shard_map.68 = (bf16[12,12,384]{2,1,0:T(8,128)(2,1)S(1)}, f32[48,4,48]{2,1,0:T(4,128)S(1)}) custom-call(s32[48]{0:T(128)} %shift_hbm.1, bf16[12,12,384]{2,1,0:T(8,128)(2,1)} %bitcast.6, bf16[144,4,384]{2,1,0:T(4,128)(2,1)} %bitcast.5, f32[96,4,384]{2,1,0:T(4,128)} %bitcast.4, s32[4,384]{1,0:T(4,128)} %near_hbm.1), custom_call_target="tpu_custom_call" | custom-call | tf_op jit(solution)/shard_map/pallas_call | solution.py:477
  14.2 0.7 %shard_map.69 = (bf16[12,12,384]{2,1,0:T(8,128)(2,1)}, f32[48,4,48]{2,1,0:T(4,128)}) custom-call(bf16[12,12,384]{2,1,0:T(8,128)(2,1)S(1)} %get-tuple-element.6.cor_ref, f32[48,4,48]{2,1,0:T(4,128)S(1)} %get-tuple-element.7.pol_ref), custom_call_target="tpu_custom_call" | custom-call | tf_op jit(solution)/shard_map/pallas_call | solution.py:529

commit v3 on v2

--- a/solution.py
+++ b/solution.py
@@ -20,18 +20,14 @@
 
 
 def segments(order, packed):
-    off = offsets(order)
+    stops = [16] + [o // 16 * 16 for o in offsets(order)[4::4]] + [packed]
     plan, start, first = [], 0, 0
-    for rows in (2, 4):
-        if rows < order and off[rows] // 16 * 16 > start:
-            stop = off[rows] // 16 * 16
-            plan.append((start, stop, first, rows))
-            start, first = stop, rows
-    middle = start + (packed - start) * 2 // 3 // 16 * 16
-    if middle > start:
-        plan.append((start, middle, first, order))
-        start, first = middle, order
-    return plan + [(start, packed, first, order)]
+    for stop in stops:
+        if stop > start:
+            final = 2 if start == 0 else order
+            plan.append((start, stop, first, final))
+            start, first = stop, final
+    return plan
 
 
 def complete(order, stop):
@@ -50,7 +46,7 @@
 def kernel(
     reach, shift_hbm, green_hbm, coup_hbm, weight_hbm, near_hbm, cor_ref, pol_ref,
     shift_ref, green_ref, coup_ref, weight_ref, near_ref, e16_ref, sig_ref,
-    g16, s16, l16, tri32, own, halo, gin, pout, pin, pacc, hots, chunks, cin, c4, g3, g3b, pscr, ab,
+    g16, s16, l16, tri32, own, halo, gin, pout, pin, pacc, hots, chunks, cin, c4, g3, pscr, cx, cp, gs, ps, ab, aw,
     load_sem, side_sem, near_sem, far_sem, halo_send, halo_recv, gin_send, gin_recv, part_send, part_recv,
     chunk_send, chunk_recv,
 ):
@@ -60,7 +56,8 @@
     freqs = shift_ref.shape[0]
     tiles = atoms // LANES
     packed = own.shape[0]
-    pad = c4.shape[3]
+    pad = c4.shape[2]
+    fold = cx.shape[3]
     ne = lax.axis_size("energy")
     nl = lax.axis_size("layer")
     me = lax.axis_index("energy")
@@ -69,14 +66,18 @@
     depth = s16.shape[1]
     off = offsets(order)
     plan = segments(order, packed)
-    groups = (tuple(range(2, nbr)), (0, 1))
+    slots = tuple(range(2, nbr))
+    size = len(slots)
 
     def load(n, src, dst):
         copy = pltpu.make_async_copy(src, dst, load_sem.at[n])
         copy.start()
         return copy
 
-    load_green = load(0, green_hbm, green_ref)
+    step = order // 4
+    for p in range(0, order, step):
+        load(0, green_hbm.at[pl.ds(p, step)], green_ref.at[pl.ds(p, step)])
+    load_green = pltpu.make_async_copy(green_hbm, green_ref, load_sem.at[0])
     load_near = load(1, near_hbm, near_ref)
     load_coup = load(2, coup_hbm, coup_ref)
     load_weight = load(3, weight_hbm, weight_ref)
@@ -115,26 +116,10 @@
         greet(barrier, me - 1, layer)
 
     tri32[...] = jnp.zeros_like(tri32)
-    e16_ref[...] = expansion(order, depth, packed)
     load_green.wait()
     for p in range(order):
         tri32[off[p] : off[p] + order - p, :] = green_ref[p].astype(F32)[p:, :]
     own[...] = tri32[...].astype(BF16)
-
-    @pl.when(jnp.logical_not(has_above & has_below))
-    def _():
-        g3b[...] = jnp.zeros_like(g3b)
-
-    for d in range(1, reach + 1):
-
-        @pl.when(me < d)
-        def _():
-            gin[d - 1] = jnp.zeros((packed, atoms), BF16)
-            pin[2 * d - 2] = jnp.zeros(pin.shape[1:], BF16)
-
-        @pl.when(me + d >= ne)
-        def _():
-            pin[2 * d - 1] = jnp.zeros(pin.shape[1:], BF16)
 
     pl.semaphore_wait(
         barrier,
@@ -211,58 +196,26 @@
         def _():
             greet(near_sem if d <= reach else far_sem, me - d, layer)
 
-    picked = (g3, g3b)
     row = lax.broadcasted_iota(jnp.int32, (atoms, atoms), 0)
 
     def one_hot(k, start):
         return jnp.where(row == near_ref[k : k + 1, :] - start, 1.0, 0.0).astype(BF16)
 
-    def pick_neighbours(g, j, blocks, hot):
-        size = len(groups[g])
+    def taken(blocks, hot):
         found = jnp.dot(blocks, hot, preferred_element_type=F32)
-        for t in range(tiles):
-            picked[g][pl.ds(t * size + j, packed, stride=pad), :] = found[
-                :, t * LANES : (t + 1) * LANES
-            ]
+        return [found[:, t * LANES : (t + 1) * LANES] for t in range(tiles)]
+
+    def pick_side(side):
+        for t, found in enumerate(taken(halo[side], hots[side])):
+            for n in range(2):
+                gs[side, pl.ds(n * tiles + t, packed, stride=fold), :] = found
 
     load_near.wait()
-    for j in range(len(groups[0])):
-        pick_neighbours(0, j, own[...], one_hot(groups[0][j], atoms))
+    for j, k in enumerate(slots):
+        for t, found in enumerate(taken(own[...], one_hot(k, atoms))):
+            g3[pl.ds(t * size + j, packed, stride=pad), :] = found
     hots[0] = one_hot(0, 0)
     hots[1] = one_hot(1, 2 * atoms)
-
-    load_coup.wait()
-    for g, slots in enumerate(groups):
-        size = len(slots)
-        for t in range(tiles):
-            block = coup_ref[:, :, t * LANES : (t + 1) * LANES].astype(F32)
-            block = block.reshape(order, order, nbr, LANES)
-            c4[g, :, :, t * size : (t + 1) * size, :] = block[
-                :, :, slots[0] : slots[0] + size, :
-            ]
-
-    last = off[-1] + 1
-    for g in range(2):
-        pscr[g, last * pad :, :] = jnp.zeros(((packed - last) * pad, LANES), F32)
-
-    def entry(g, low, high):
-        at = (off[low] + high - low) * pad
-        return picked[g][at : at + pad, :]
-
-    def products(g, start, stop):
-        for i in range(start, stop, 2):
-            first = jnp.zeros((2, order, pad, LANES), F32)
-            for p in range(order):
-                block = jnp.stack([entry(g, min(p, q), max(p, q)) for q in range(order)])
-                first = first + c4[g, i : i + 2, p][:, None] * block[None]
-            total = first[:, 0][:, None] * c4[g, i:, 0][None]
-            for q in range(1, order):
-                total = total + first[:, q][:, None] * c4[g, i:, q][None]
-            total = total.astype(BF16).astype(F32)
-            for n in range(2):
-                pscr[g, off[i + n] * pad : (off[i + n] + order - i - n) * pad, :] = total[
-                    n, n:
-                ].reshape(-1, LANES)
 
     @pl.when(even & has_above)
     def _():
@@ -279,7 +232,83 @@
         def _():
             green_copy(d).start()
 
-    products(0, 0, order)
+    both = has_above & has_below
+    lower_first = lax.rem(layer, 2) == 1
+    early = jnp.where(both, jnp.where(lower_first, 0, 1), jnp.where(has_above, 0, 1))
+    late = 1 - early
+
+    @pl.when(jnp.logical_not(both))
+    def _():
+        ps[early] = jnp.zeros(ps.shape[1:], F32)
+
+    for d in range(1, reach + 1):
+
+        @pl.when(me < d)
+        def _():
+            gin[d - 1] = jnp.zeros((packed, atoms), BF16)
+            pin[2 * d - 2] = jnp.zeros(pin.shape[1:], BF16)
+
+        @pl.when(me + d >= ne)
+        def _():
+            pin[2 * d - 1] = jnp.zeros(pin.shape[1:], BF16)
+
+    e16_ref[...] = expansion(order, depth, packed)
+    load_coup.wait()
+    for t in range(tiles):
+        block = coup_ref[:, :, t * LANES : (t + 1) * LANES].astype(F32)
+        block = block.reshape(order, order, nbr, LANES)
+        c4[:, :, t * size : (t + 1) * size, :] = block[:, :, slots[0] :, :]
+        for side in range(2):
+            for n in range(2):
+                at = n * tiles + t
+                cx[side, :, :, at : at + 1, :] = block[:, :, side : side + 1, :]
+    lower = lax.broadcasted_iota(jnp.int32, (order, fold, LANES), 1) < tiles
+    for side in range(2):
+        for i in range(0, order, 2):
+            cp[side, i // 2] = jnp.where(lower, cx[side, i], cx[side, i + 1])
+
+    last = off[-1] + 1
+    pscr[last * pad :, :] = jnp.zeros(((packed - last) * pad, LANES), F32)
+    for side in range(2):
+        ps[side, last * fold :, :] = jnp.zeros(((packed - last) * fold, LANES), F32)
+
+    def entries(p, rows):
+        at = [off[min(p, q)] + abs(p - q) for q in range(order)]
+        return [slice(a * rows, (a + 1) * rows) for a in at]
+
+    def products():
+        for i in range(0, order, 2):
+            first = jnp.zeros((2, order, pad, LANES), F32)
+            for p in range(order):
+                block = jnp.stack([g3[at, :] for at in entries(p, pad)])
+                first = first + c4[i : i + 2, p][:, None] * block[None]
+            total = first[:, 0][:, None] * c4[i:, 0][None]
+            for q in range(1, order):
+                total = total + first[:, q][:, None] * c4[i:, q][None]
+            total = total.astype(BF16).astype(F32)
+            for n in range(2):
+                pscr[off[i + n] * pad : (off[i + n] + order - i - n) * pad, :] = total[
+                    n, n:
+                ].reshape(-1, LANES)
+
+    def side_products(side, start, stop):
+        for i in range(start, stop, 2):
+            first = jnp.zeros((order, fold, LANES), F32)
+            for p in range(order):
+                block = jnp.stack([gs[side, at, :] for at in entries(p, fold)])
+                first = first + cp[side, i // 2, p][None] * block
+            total = first[0][None] * cx[side, i:, 0]
+            for q in range(1, order):
+                total = total + first[q][None] * cx[side, i:, q]
+            total = total.astype(BF16).astype(F32).reshape(-1, LANES)
+            ps[side, off[i] * fold : off[i + 1] * fold, :] = total
+            second = total[fold:].reshape(-1, fold, LANES)
+            second = jnp.concatenate([second[:, tiles:], second[:, :tiles]], axis=1)
+            ps[side, off[i + 1] * fold : (off[i + 1] + order - i - 1) * fold, :] = second.reshape(
+                -1, LANES
+            )
+
+    products()
 
     load_weight.wait()
     load_shift.wait()
@@ -299,38 +328,60 @@
     )
     for s in range(2 * reach):
         ab[s] = sums[s]
-
-    def rows_of(g, t, j, start, stop):
-        at = start * pad + t * len(groups[g]) + j
-        return pscr[g, pl.ds(at, stop - start, stride=pad), :]
-
-    def partials(g, t, s, start, stop):
+        for side in range(2):
+            aw[side, s] = jnp.broadcast_to(sums[s][side : side + 1], aw.shape[2:])
+
+    def rows_of(j, t, start, stop):
+        at = start * pad + t * size + j
+        return pscr[pl.ds(at, stop - start, stride=pad), :]
+
+    def side_rows(side, t, start, stop):
+        return ps[side, pl.ds(start * fold + t, stop - start, stride=fold), :]
+
+    def side_partials(side, t, s, start, stop):
         lanes = slice(t * LANES, (t + 1) * LANES)
-        total = None
-        for j, k in enumerate(groups[g]):
-            term = ab[s, k : k + 1, lanes] * rows_of(g, t, j, start, stop)
-            total = term if total is None else total + term
-        return total
+        weight = aw[side, s, 0:1, lanes]
+        return pacc[s, start:stop, lanes] + weight * side_rows(side, t, start, stop)
 
     for t in range(tiles):
+        lanes = slice(t * LANES, (t + 1) * LANES)
         for s in range(2 * reach):
-            pacc[s, :, t * LANES : (t + 1) * LANES] = partials(0, t, s, 0, packed)
+            total = None
+            for j, k in enumerate(slots):
+                term = ab[s, k : k + 1, lanes] * rows_of(j, t, 0, packed)
+                total = term if total is None else total + term
+            pacc[s, :, lanes] = total
 
     g16[...] = jnp.zeros_like(g16)
     for p in range(order):
         g16[p, :order, :] = green_ref[p].astype(F32)
     sig_ref[...] = jnp.zeros_like(sig_ref)
 
-    @pl.when(has_above)
+    @pl.when(both & lower_first)
+    def _():
+        halo_copy(0).wait_recv()
+
+    @pl.when(both & jnp.logical_not(lower_first))
     def _():
         halo_copy(1).wait_recv()
-        pick_neighbours(1, 1, halo[1], hots[1])
-
-    @pl.when(has_below)
+
+    @pl.when(both)
+    def _():
+        pick_side(early)
+        side_products(early, 0, order)
+        for t in range(tiles):
+            for s in range(2 * reach):
+                pacc[s, :, t * LANES : (t + 1) * LANES] = side_partials(early, t, s, 0, packed)
+
+    @pl.when(late == 0)
     def _():
         halo_copy(0).wait_recv()
-        pick_neighbours(1, 0, halo[0], hots[0])
-
+
+    @pl.when(late == 1)
+    def _():
+        halo_copy(1).wait_recv()
+
+    pick_side(late)
 
     send_order = [(1 - 2 * (d % 2 == 0)) * d for d in range(1, reach + 1)]
     send_order += [-d for d in send_order]
@@ -348,21 +399,18 @@
             twice = jnp.where(index == off[p], 1.0, twice)
         rows = [[None] * tiles for _ in range(reach * nbr)]
 
-        def correlate(g, start, stop):
-            for t in range(tiles):
-                lanes = slice(t * LANES, (t + 1) * LANES)
-                greens = [
-                    gin[d, start:stop, lanes].astype(F32) * twice[start:stop] for d in range(reach)
-                ]
-                for j, k in enumerate(groups[g]):
-                    value = rows_of(g, t, j, start, stop)
-                    for d in range(reach):
-                        term = jnp.sum(greens[d] * value, axis=0, keepdims=True)
-                        old = rows[d * nbr + k][t]
-                        rows[d * nbr + k][t] = term if old is None else old + term
-
-        correlate(0, 0, packed)
-        correlate(1, 0, packed)
+        for t in range(tiles):
+            greens = [
+                gin[d, :, t * LANES : (t + 1) * LANES].astype(F32) * twice for d in range(reach)
+            ]
+            for k in range(nbr):
+                if k < 2:
+                    value = side_rows(k, t, 0, packed)
+                else:
+                    value = rows_of(k - 2, t, 0, packed)
+                for d in range(reach):
+                    rows[d * nbr + k][t] = jnp.sum(greens[d] * value, axis=0, keepdims=True)
+
         sums = [jnp.concatenate([r[t] for r in rows], axis=0) for t in range(tiles)]
         lane = lax.broadcasted_iota(jnp.int32, sums[0].shape, 1)
         for e in range(ne):
@@ -374,14 +422,13 @@
 
     for n, (start, stop, first, final) in enumerate(plan):
         if first < final:
-            products(1, first, final)
+            side_products(late, first, final)
             if final == order:
                 correlations()
         for t in range(tiles):
             lanes = slice(t * LANES, (t + 1) * LANES)
             for s in range(2 * reach):
-                total = pacc[s, start:stop, lanes] + partials(1, t, s, start, stop)
-                pout[s, start:stop, lanes] = total.astype(BF16)
+                pout[s, start:stop, lanes] = side_partials(late, t, s, start, stop).astype(BF16)
         for d in send_order:
             if d > 0:
 
@@ -467,7 +514,8 @@
     share = atoms // ne
     count = order * (order + 1) // 2
     packed = -(-count // 16) * 16
-    pad = -(-(tiles * max(nbr - 2, 2)) // 8) * 8
+    pad = -(-(tiles * (nbr - 2)) // 8) * 8
+    fold = -(-(2 * tiles) // 8) * 8
     rows = 16 * (-(-order // 16))
     parts = len(segments(order, packed))
     vmem = pl.BlockSpec(memory_space=pltpu.VMEM)
@@ -503,11 +551,15 @@
             pltpu.VMEM((2, atoms, atoms), BF16),
             pltpu.VMEM((ne, reach * nbr, LANES), F32),
             pltpu.VMEM((ne, reach * nbr, LANES), F32),
-            pltpu.VMEM((2, order, order, pad, LANES), F32),
+            pltpu.VMEM((order, order, pad, LANES), F32),
             pltpu.VMEM((packed * pad, LANES), F32),
             pltpu.VMEM((packed * pad, LANES), F32),
-            pltpu.VMEM((2, packed * pad, LANES), F32),
+            pltpu.VMEM((2, order, order, fold, LANES), F32),
+            pltpu.VMEM((2, order // 2, order, fold, LANES), F32),
+            pltpu.VMEM((2, packed * fold, LANES), F32),
+            pltpu.VMEM((2, packed * fold, LANES), F32),
             pltpu.VMEM((2 * reach, nbr, atoms), F32),
+            pltpu.VMEM((2, 2 * reach, 8, atoms), F32),
             dma((5,)), *[pltpu.SemaphoreType.REGULAR] * 3,
             dma((1,)), dma((2,)), dma((1,)), dma((1,)), dma((1,)), dma((parts,)), dma((1,)), dma((1,)),
         ],

time: 15.1 us -> 14.7 us (0.974)
  the two profiles are of different devices: /device:TPU:0 before, /device:TPU:13 now
where the time goes in v3:
time: 14.7 us; the launch traced here: 14.6 us
  Pallas kernels  13.9 us (95%)
  between operations  0.64 us (4%)
    pallas_call x1, Pallas kernels, body(): pl.pallas_call(functools.partial(kernel, reach), out_shape=(jax.ShapeDtyp...  13.2 us
    pallas_call x1, Pallas kernels, body(): pl.pallas_call(finish, out_shape=(jax.ShapeDtypeStruct((order, order, ato...  0.71 us

profile of v3, /device:TPU:13, one launch (start us, length us, event | category | flops | bytes accessed | tf_op | source)
XLA Modules:
  0.0 14.6 jit_solution(17566346516952497220)
XLA Ops:
  0.6 13.2 %shard_map.68 = (bf16[12,12,384]{2,1,0:T(8,128)(2,1)S(1)}, f32[48,4,48]{2,1,0:T(4,128)S(1)}) custom-call(s32[48]{0:T(128)} %shift_hbm.1, bf16[12,12,384]{2,1,0:T(8,128)(2,1)} %bitcast.6, bf16[144,4,384]{2,1,0:T(4,128)(2,1)} %bitcast.5, f32[96,4,384]{2,1,0:T(4,128)} %bitcast.4, s32[4,384]{1,0:T(4,128)} %near_hbm.1), custom_call_target="tpu_custom_call" | custom-call | tf_op jit(solution)/shard_map/pallas_call | solution.py:525
  13.9 0.7 %shard_map.69 = (bf16[12,12,384]{2,1,0:T(8,128)(2,1)}, f32[48,4,48]{2,1,0:T(4,128)}) custom-call(bf16[12,12,384]{2,1,0:T(8,128)(2,1)S(1)} %get-tuple-element.6.cor_ref, f32[48,4,48]{2,1,0:T(4,128)S(1)} %get-tuple-element.7.pol_ref), custom_call_target="tpu_custom_call" | custom-call | tf_op jit(solution)/shard_map/pallas_call | solution.py:581

commit v4 on v3

--- a/solution.py
+++ b/solution.py
@@ -30,6 +30,21 @@
     return plan
 
 
+def routes(reach):
+    straight, shared = ([], []), []
+    for d in range(1, (reach + 1) // 2 + 1):
+        for way in (1, -1):
+            slot = 2 * d - (way > 0)
+            for parity in range(2):
+                far = [abs(2 * d * way + parity - p) for p in range(2)]
+                near = [p for p in range(2) if far[p] <= reach]
+                if len(near) == 2:
+                    shared.append((2 * d * way + parity, slot))
+                elif near:
+                    straight[near[0]].append((2 * d * way + parity - near[0], slot))
+    return straight, shared
+
+
 def complete(order, stop):
     return sum(o + order - p <= stop for p, o in enumerate(offsets(order)))
 
@@ -46,8 +61,8 @@
 def kernel(
     reach, shift_hbm, green_hbm, coup_hbm, weight_hbm, near_hbm, cor_ref, pol_ref,
     shift_ref, green_ref, coup_ref, weight_ref, near_ref, e16_ref, sig_ref,
-    g16, s16, l16, tri32, own, halo, gin, pout, pin, pacc, hots, chunks, cin, c4, g3, pscr, cx, cp, gs, ps, ab, aw,
-    load_sem, side_sem, near_sem, far_sem, halo_send, halo_recv, gin_send, gin_recv, part_send, part_recv,
+    g16, s16, l16, tri32, own, halo, gin, pout, pin, given, landing, pacc, hots, chunks, cin, c4, g3, pscr, cx, cp, gs, ps, ab, aw,
+    load_sem, side_sem, near_sem, far_sem, sent_sem, halo_recv, gin_recv, part_recv, share_recv,
     chunk_send, chunk_recv,
 ):
     order = green_ref.shape[0]
@@ -79,9 +94,7 @@
         load(0, green_hbm.at[pl.ds(p, step)], green_ref.at[pl.ds(p, step)])
     load_green = pltpu.make_async_copy(green_hbm, green_ref, load_sem.at[0])
     load_near = load(1, near_hbm, near_ref)
-    load_coup = load(2, coup_hbm, coup_ref)
-    load_weight = load(3, weight_hbm, weight_ref)
-    load_shift = load(4, shift_hbm, shift_ref)
+    load_shift = load(2, shift_hbm, shift_ref)
 
     barrier = pltpu.get_barrier_semaphore()
 
@@ -92,31 +105,34 @@
 
     odd = lax.rem(me, 2) == 1
     even = jnp.logical_not(odd)
+    relayed = me >= ne - 2
+    told = even & relayed
     has_above, has_below = layer < nl - 1, layer > 0
     near_above = jnp.minimum(ne - 1 - me, reach)
     near_count = near_above + jnp.minimum(me, reach)
     far_above = ne - 1 - me - near_above
 
+    @pl.when(has_below)
+    def _():
+        greet(barrier, me + told.astype(jnp.int32), layer - 1)
+
+    @pl.when(odd)
+    def _():
+        greet(barrier, me - 1, layer)
+
+    @pl.when(has_above)
+    def _():
+        greet(barrier, me, layer + 1)
+
     for d in range(1, ne):
 
         @pl.when(me + d < ne)
         def _():
             greet(barrier, me + d, layer)
 
-    @pl.when(has_above)
-    def _():
-        greet(barrier, me, layer + 1)
-
-    @pl.when(has_below)
-    def _():
-        greet(barrier, me - lax.rem(me, 2) + 1, layer - 1)
-
-    @pl.when(odd)
-    def _():
-        greet(barrier, me - 1, layer)
-
     tri32[...] = jnp.zeros_like(tri32)
     load_green.wait()
+    load_coup = load(0, coup_hbm, coup_ref)
     for p in range(order):
         tri32[off[p] : off[p] + order - p, :] = green_ref[p].astype(F32)[p:, :]
     own[...] = tri32[...].astype(BF16)
@@ -126,7 +142,7 @@
         me
         + even.astype(jnp.int32)
         + has_below.astype(jnp.int32)
-        + 2 * (odd & has_above).astype(jnp.int32),
+        + jnp.where(told, 0, jnp.where(relayed, 2, 1)) * has_above.astype(jnp.int32),
     )
 
     def remote(src, dst, send, recv, energy, row):
@@ -135,22 +151,58 @@
             device_id={"energy": energy, "layer": row}, device_id_type=MESH,
         )
 
+    straight, shared = routes(reach)
+    base = me - lax.rem(me, 2)
+
+    def reaches(offset):
+        return (offset >= 0) & (offset < ne)
+
+    def heard(slot):
+        d = (slot + 1) // 2
+        if slot % 2:
+            return (base >= 2 * d) & (2 * d - even.astype(jnp.int32) <= reach)
+        return (base + 2 * d < ne) & (2 * d - odd.astype(jnp.int32) <= reach)
+
+    def number(conditions):
+        total = 0
+        for condition in conditions:
+            total = total + condition.astype(jnp.int32)
+        return total
+
+    heard_count = 1 + number([heard(slot) for slot in range(1, pin.shape[0])])
+    shared_count = number([reaches(base + e) for e, _ in shared])
+    sent_count = 1 + shared_count + near_above + number([has_above, has_below])
+    for parity in range(2):
+        which = odd if parity else even
+        sent_count = sent_count + number([which & reaches(me + e) for e, _ in straight[parity]])
+
     def halo_copy(side):
         row = layer + 1 if side == 0 else layer - 1
-        return remote(own, halo.at[side], halo_send.at[0], halo_recv.at[side], me, row)
+        return remote(own, halo.at[side], sent_sem.at[0], halo_recv.at[side], me, row)
 
     def green_copy(d):
         return remote(
-            own, gin.at[d - 1], gin_send.at[0], gin_recv.at[0], me + d, layer
-        )
-
-    def part_copy(slot, n, energy):
+            own, gin.at[d - 1], sent_sem.at[0], gin_recv.at[0], me + d, layer
+        )
+
+    def part_copy(source, target, n, e):
         start, stop, _, _ = plan[n]
         rows = pl.ds(start, stop - start)
         return remote(
-            pout.at[slot, rows], pin.at[slot, rows], part_send.at[0], part_recv.at[n],
-            energy, layer,
-        )
+            pout.at[source, rows], target.at[rows], sent_sem.at[0],
+            part_recv.at[n], me + e, layer,
+        )
+
+    def share_copy(source, number, n):
+        start, stop, _, _ = plan[n]
+        rows = pl.ds(start, stop - start)
+        return remote(
+            pout.at[source, rows], given.at[number, rows], sent_sem.at[0], share_recv.at[n],
+            me + 1, layer,
+        )
+
+    def outgoing(offset):
+        return 2 * offset - 2 if offset > 0 else -2 * offset - 1
 
     def chunk_copy(r):
         dest = lax.rem(me + r, ne)
@@ -158,24 +210,44 @@
             chunks.at[dest], cin.at[r], chunk_send.at[0], chunk_recv.at[0], dest, layer
         )
 
-    def wait_gin(send):
-        number = jnp.minimum(ne - 1 - me, reach) if send else jnp.minimum(me, reach)
+    def wait_gin():
         for c in range(1, reach + 1):
 
-            @pl.when(number == c)
+            @pl.when(jnp.minimum(me, reach) == c)
             def _():
                 some = gin.at[pl.ds(0, c)]
-                copy = remote(some, some, gin_send.at[0], gin_recv.at[0], me, layer)
-                copy.wait_send() if send else copy.wait_recv()
-
-    def wait_parts(rows, recv, send):
-        for c in range(1, 2 * reach + 1):
-
-            @pl.when(near_count == c)
+                remote(some, some, sent_sem.at[0], gin_recv.at[0], me, layer).wait_recv()
+
+    def wait_parts(count, most, rows, copy_of):
+        for c in range(1, most + 1):
+
+            @pl.when(count == c)
             def _():
-                some = pin.at[pl.ds(0, c), rows]
-                copy = remote(some, some, part_send.at[0], part_recv.at[recv], me, layer)
-                copy.wait_send() if send else copy.wait_recv()
+                copy_of(landing.at[pl.ds(0, c), rows])
+
+    def wait_heard(rows, n):
+        wait_parts(
+            heard_count, pin.shape[0], rows,
+            lambda some: remote(
+                some, some, sent_sem.at[0], part_recv.at[n], me, layer
+            ).wait_recv(),
+        )
+
+    def wait_shared(rows, n):
+        wait_parts(
+            shared_count, len(shared), rows,
+            lambda some: remote(
+                some, some, sent_sem.at[0], share_recv.at[n], me, layer
+            ).wait_recv(),
+        )
+
+    def wait_sent():
+        wait_parts(
+            sent_count, landing.shape[0], pl.ds(0, packed),
+            lambda some: remote(
+                some, some, sent_sem.at[0], part_recv.at[0], me, layer
+            ).wait_send(),
+        )
 
     def wait_chunks():
         some = cin.at[pl.ds(1, ne - 1)]
@@ -185,9 +257,12 @@
     def _():
         halo_copy(1).start()
 
-    @pl.when(odd & has_above)
+    @pl.when(has_above & jnp.logical_not(told))
     def _():
         halo_copy(0).start()
+
+    @pl.when(has_above & odd & relayed)
+    def _():
         greet(side_sem, me - 1, layer)
 
     for d in range(1, ne):
@@ -211,13 +286,14 @@
                 gs[side, pl.ds(n * tiles + t, packed, stride=fold), :] = found
 
     load_near.wait()
+    load_weight = load(1, weight_hbm, weight_ref)
     for j, k in enumerate(slots):
         for t, found in enumerate(taken(own[...], one_hot(k, atoms))):
             g3[pl.ds(t * size + j, packed, stride=pad), :] = found
     hots[0] = one_hot(0, 0)
     hots[1] = one_hot(1, 2 * atoms)
 
-    @pl.when(even & has_above)
+    @pl.when(told & has_above)
     def _():
         pl.semaphore_wait(side_sem, 1)
         halo_copy(0).start()
@@ -246,11 +322,12 @@
         @pl.when(me < d)
         def _():
             gin[d - 1] = jnp.zeros((packed, atoms), BF16)
-            pin[2 * d - 2] = jnp.zeros(pin.shape[1:], BF16)
-
-        @pl.when(me + d >= ne)
+
+    for slot in range(1, pin.shape[0]):
+
+        @pl.when(jnp.logical_not(heard(slot)))
         def _():
-            pin[2 * d - 1] = jnp.zeros(pin.shape[1:], BF16)
+            pin[slot] = jnp.zeros(pin.shape[1:], BF16)
 
     e16_ref[...] = expansion(order, depth, packed)
     load_coup.wait()
@@ -383,15 +460,12 @@
 
     pick_side(late)
 
-    send_order = [(1 - 2 * (d % 2 == 0)) * d for d in range(1, reach + 1)]
-    send_order += [-d for d in send_order]
-
     def correlations():
         @pl.when(far_above > 0)
         def _():
             pl.semaphore_wait(far_sem, far_above)
 
-        wait_gin(False)
+        wait_gin()
 
         index = lax.broadcasted_iota(jnp.int32, (packed, LANES), 0)
         twice = jnp.full((packed, LANES), 2.0, F32)
@@ -424,28 +498,61 @@
         if first < final:
             side_products(late, first, final)
             if final == order:
-                correlations()
+                pl.when(me >= ne // 2)(correlations)
         for t in range(tiles):
             lanes = slice(t * LANES, (t + 1) * LANES)
             for s in range(2 * reach):
                 pout[s, start:stop, lanes] = side_partials(late, t, s, start, stop).astype(BF16)
-        for d in send_order:
-            if d > 0:
-
-                @pl.when(me + d < ne)
+
+        @pl.when(even)
+        def _():
+            for e, slot in straight[0]:
+
+                @pl.when(reaches(me + e))
                 def _():
-                    part_copy(2 * d - 2, n, me + d).start()
-            else:
-
-                @pl.when(me >= -d)
+                    part_copy(outgoing(e), pin.at[slot], n, e).start()
+
+            for number, (e, _) in enumerate(shared):
+
+                @pl.when(reaches(me + e))
                 def _():
-                    part_copy(-2 * d - 1, n, me + d).start()
+                    share_copy(outgoing(e), number, n).start()
+
+            part_copy(outgoing(1), pin.at[0], n, 1).start()
+
+        @pl.when(odd)
+        def _():
+            for e, slot in straight[1]:
+
+                @pl.when(reaches(me + e))
+                def _():
+                    part_copy(outgoing(e), pin.at[slot], n, e).start()
+
+            part_copy(outgoing(-1), pin.at[0], n, -1).start()
+
+    pl.when(me < ne // 2)(correlations)
+
+    @pl.when(odd)
+    def _():
+        for n, (start, stop, _, _) in enumerate(plan):
+            wait_shared(pl.ds(start, stop - start), n)
+            for number, (e, slot) in enumerate(shared):
+                out = outgoing(e - 1)
+
+                @pl.when(reaches(base + e))
+                def _():
+                    for t in range(tiles):
+                        lanes = slice(t * LANES, (t + 1) * LANES)
+                        total = side_partials(late, t, out, start, stop)
+                        total = total + given[number, start:stop, lanes].astype(F32)
+                        pout[out, start:stop, lanes] = total.astype(BF16)
+                    part_copy(out, pin.at[slot], n, e - 1).start()
 
     for n, (start, stop, _, _) in enumerate(plan):
         first, final = complete(order, start), complete(order, stop)
-        wait_parts(pl.ds(start, stop - start), n, False)
+        wait_heard(pl.ds(start, stop - start), n)
         sigma = pin[0, start:stop].astype(F32)
-        for s in range(1, 2 * reach):
+        for s in range(1, pin.shape[0]):
             sigma = sigma + pin[s, start:stop].astype(F32)
         sig_ref[start:stop, :] = sigma.astype(BF16)
         s16[first:final] = jnp.dot(
@@ -482,15 +589,7 @@
             value = jnp.where(shift == d, summed[(d - 1) * nbr : d * nbr], value)
         pol_ref[w] = value
 
-    for c in range(1, 3):
-
-        @pl.when(has_above.astype(jnp.int32) + has_below.astype(jnp.int32) == c)
-        def _():
-            some = halo.at[pl.ds(0, c)]
-            remote(some, some, halo_send.at[0], halo_recv.at[0], me, layer).wait_send()
-
-    wait_gin(True)
-    wait_parts(pl.ds(0, packed), 0, True)
+    wait_sent()
     wait_chunks().wait_send()
 
 
@@ -546,7 +645,9 @@
             pltpu.VMEM((2, packed, atoms), BF16),
             pltpu.VMEM((reach, packed, atoms), BF16),
             pltpu.VMEM((2 * reach, packed, atoms), BF16),
-            pltpu.VMEM((2 * reach, packed, atoms), BF16),
+            pltpu.VMEM((1 + 2 * ((reach + 1) // 2), packed, atoms), BF16),
+            pltpu.VMEM((max(len(routes(reach)[1]), 1), packed, atoms), BF16),
+            pltpu.VMEM((4 + 3 * reach, packed, atoms), BF16),
             pltpu.VMEM((2 * reach, packed, atoms), F32),
             pltpu.VMEM((2, atoms, atoms), BF16),
             pltpu.VMEM((ne, reach * nbr, LANES), F32),
@@ -560,8 +661,8 @@
             pltpu.VMEM((2, packed * fold, LANES), F32),
             pltpu.VMEM((2 * reach, nbr, atoms), F32),
             pltpu.VMEM((2, 2 * reach, 8, atoms), F32),
-            dma((5,)), *[pltpu.SemaphoreType.REGULAR] * 3,
-            dma((1,)), dma((2,)), dma((1,)), dma((1,)), dma((1,)), dma((parts,)), dma((1,)), dma((1,)),
+            dma((3,)), *[pltpu.SemaphoreType.REGULAR] * 3,
+            dma((1,)), dma((2,)), dma((1,)), dma((parts,)), dma((parts,)), dma((1,)), dma((1,)),
         ],
         compiler_params=pltpu.CompilerParams(
             collective_id=0, has_side_effects=True, vmem_limit_bytes=VMEM_LIMIT

time: 14.7 us -> 14.5 us (0.986)
  the two profiles are of different devices: /device:TPU:13 before, /device:TPU:0 now
where the time goes in v4:
time: 14.5 us; the launch traced here: 14.3 us
  Pallas kernels  13.6 us (94%)
  between operations  0.64 us (4%)
    pallas_call x1, Pallas kernels, body(): pl.pallas_call(functools.partial(kernel, reach), out_shape=(jax.ShapeDtyp...  12.9 us
    pallas_call x1, Pallas kernels, body(): pl.pallas_call(finish, out_shape=(jax.ShapeDtypeStruct((order, order, ato...  0.71 us

profile of v4, /device:TPU:0, one launch (start us, length us, event | category | flops | bytes accessed | tf_op | source)
XLA Modules:
  0.0 14.3 jit_solution(4343247271527688500)
XLA Ops:
  0.6 12.9 %shard_map.68 = (bf16[12,12,384]{2,1,0:T(8,128)(2,1)S(1)}, f32[48,4,48]{2,1,0:T(4,128)S(1)}) custom-call(s32[48]{0:T(128)} %shift_hbm.1, bf16[12,12,384]{2,1,0:T(8,128)(2,1)} %bitcast.6, bf16[144,4,384]{2,1,0:T(4,128)(2,1)} %bitcast.5, f32[96,4,384]{2,1,0:T(4,128)} %bitcast.4, s32[4,384]{1,0:T(4,128)} %near_hbm.1), custom_call_target="tpu_custom_call" | custom-call | tf_op jit(solution)/shard_map/pallas_call | solution.py:624
  13.6 0.7 %shard_map.69 = (bf16[12,12,384]{2,1,0:T(8,128)(2,1)}, f32[48,4,48]{2,1,0:T(4,128)}) custom-call(bf16[12,12,384]{2,1,0:T(8,128)(2,1)S(1)} %get-tuple-element.6.cor_ref, f32[48,4,48]{2,1,0:T(4,128)S(1)} %get-tuple-element.7.pol_ref), custom_call_target="tpu_custom_call" | custom-call | tf_op jit(solution)/shard_map/pallas_call | solution.py:682

commit v5 on v4

--- a/solution.py
+++ b/solution.py
@@ -20,7 +20,7 @@
 
 
 def segments(order, packed):
-    stops = [16] + [o // 16 * 16 for o in offsets(order)[4::4]] + [packed]
+    stops = [16] + [o // 16 * 16 for o in offsets(order)[8::4]] + [packed]
     plan, start, first = [], 0, 0
     for stop in stops:
         if stop > start:
@@ -185,19 +185,22 @@
             own, gin.at[d - 1], sent_sem.at[0], gin_recv.at[0], me + d, layer
         )
 
-    def part_copy(source, target, n, e):
-        start, stop, _, _ = plan[n]
+    arrivals = [(0, plan[1][1])] + [(start, stop) for start, stop, _, _ in plan[2:]]
+
+    def group(start):
+        return sum(start >= stop for _, stop in arrivals)
+
+    def part_copy(source, target, start, stop, e):
         rows = pl.ds(start, stop - start)
         return remote(
             pout.at[source, rows], target.at[rows], sent_sem.at[0],
-            part_recv.at[n], me + e, layer,
-        )
-
-    def share_copy(source, number, n):
-        start, stop, _, _ = plan[n]
+            part_recv.at[group(start)], me + e, layer,
+        )
+
+    def share_copy(source, number, start, stop):
         rows = pl.ds(start, stop - start)
         return remote(
-            pout.at[source, rows], given.at[number, rows], sent_sem.at[0], share_recv.at[n],
+            pout.at[source, rows], given.at[number, rows], sent_sem.at[0], share_recv.at[group(start)],
             me + 1, layer,
         )
 
@@ -510,15 +513,15 @@
 
                 @pl.when(reaches(me + e))
                 def _():
-                    part_copy(outgoing(e), pin.at[slot], n, e).start()
+                    part_copy(outgoing(e), pin.at[slot], start, stop, e).start()
 
             for number, (e, _) in enumerate(shared):
 
                 @pl.when(reaches(me + e))
                 def _():
-                    share_copy(outgoing(e), number, n).start()
-
-            part_copy(outgoing(1), pin.at[0], n, 1).start()
+                    share_copy(outgoing(e), number, start, stop).start()
+
+            part_copy(outgoing(1), pin.at[0], start, stop, 1).start()
 
         @pl.when(odd)
         def _():
@@ -526,15 +529,15 @@
 
                 @pl.when(reaches(me + e))
                 def _():
-                    part_copy(outgoing(e), pin.at[slot], n, e).start()
-
-            part_copy(outgoing(-1), pin.at[0], n, -1).start()
+                    part_copy(outgoing(e), pin.at[slot], start, stop, e).start()
+
+            part_copy(outgoing(-1), pin.at[0], start, stop, -1).start()
 
     pl.when(me < ne // 2)(correlations)
 
     @pl.when(odd)
     def _():
-        for n, (start, stop, _, _) in enumerate(plan):
+        for n, (start, stop) in enumerate(arrivals):
             wait_shared(pl.ds(start, stop - start), n)
             for number, (e, slot) in enumerate(shared):
                 out = outgoing(e - 1)
@@ -546,9 +549,9 @@
                         total = side_partials(late, t, out, start, stop)
                         total = total + given[number, start:stop, lanes].astype(F32)
                         pout[out, start:stop, lanes] = total.astype(BF16)
-                    part_copy(out, pin.at[slot], n, e - 1).start()
-
-    for n, (start, stop, _, _) in enumerate(plan):
+                    part_copy(out, pin.at[slot], start, stop, e - 1).start()
+
+    for n, (start, stop) in enumerate(arrivals):
         first, final = complete(order, start), complete(order, stop)
         wait_heard(pl.ds(start, stop - start), n)
         sigma = pin[0, start:stop].astype(F32)
@@ -616,7 +619,7 @@
     pad = -(-(tiles * (nbr - 2)) // 8) * 8
     fold = -(-(2 * tiles) // 8) * 8
     rows = 16 * (-(-order // 16))
-    parts = len(segments(order, packed))
+    parts = len(segments(order, packed)) - 1
     vmem = pl.BlockSpec(memory_space=pltpu.VMEM)
     hbm = pl.BlockSpec(memory_space=pltpu.HBM)
     dma = pltpu.SemaphoreType.DMA

time: 14.5 us -> 14.5 us (level)
  no operation moved by 1% of the time
where the time goes in v5:
time: 14.5 us; the launch traced here: 14.2 us
  Pallas kernels  13.6 us (94%)
  between operations  0.64 us (4%)
    pallas_call x1, Pallas kernels, body(): pl.pallas_call(functools.partial(kernel, reach), out_shape=(jax.ShapeDtyp...  12.9 us
    pallas_call x1, Pallas kernels, body(): pl.pallas_call(finish, out_shape=(jax.ShapeDtypeStruct((order, order, ato...  0.71 us

profile of v5, /device:TPU:0, one launch (start us, length us, event | category | flops | bytes accessed | tf_op | source)
XLA Modules:
  0.0 14.2 jit_solution(2630646178438375427)
XLA Ops:
  0.6 12.9 %shard_map.68 = (bf16[12,12,384]{2,1,0:T(8,128)(2,1)S(1)}, f32[48,4,48]{2,1,0:T(4,128)S(1)}) custom-call(s32[48]{0:T(128)} %shift_hbm.1, bf16[12,12,384]{2,1,0:T(8,128)(2,1)} %bitcast.6, bf16[144,4,384]{2,1,0:T(4,128)(2,1)} %bitcast.5, f32[96,4,384]{2,1,0:T(4,128)} %bitcast.4, s32[4,384]{1,0:T(4,128)} %near_hbm.1), custom_call_target="tpu_custom_call" | custom-call | tf_op jit(solution)/shard_map/pallas_call | solution.py:627
  13.5 0.7 %shard_map.69 = (bf16[12,12,384]{2,1,0:T(8,128)(2,1)}, f32[48,4,48]{2,1,0:T(4,128)}) custom-call(bf16[12,12,384]{2,1,0:T(8,128)(2,1)S(1)} %get-tuple-element.6.cor_ref, f32[48,4,48]{2,1,0:T(4,128)S(1)} %get-tuple-element.7.pol_ref), custom_call_target="tpu_custom_call" | custom-call | tf_op jit(solution)/shard_map/pallas_call | solution.py:685

commit v6 on v5

--- a/solution.py
+++ b/solution.py
@@ -94,7 +94,6 @@
         load(0, green_hbm.at[pl.ds(p, step)], green_ref.at[pl.ds(p, step)])
     load_green = pltpu.make_async_copy(green_hbm, green_ref, load_sem.at[0])
     load_near = load(1, near_hbm, near_ref)
-    load_shift = load(2, shift_hbm, shift_ref)
 
     barrier = pltpu.get_barrier_semaphore()
 
@@ -334,6 +333,7 @@
 
     e16_ref[...] = expansion(order, depth, packed)
     load_coup.wait()
+    load_shift = load(0, shift_hbm, shift_ref)
     for t in range(tiles):
         block = coup_ref[:, :, t * LANES : (t + 1) * LANES].astype(F32)
         block = block.reshape(order, order, nbr, LANES)
@@ -587,8 +587,8 @@
     summed = summed[:, :share] * (1.0 / (order * math.sqrt(ne)))
     for w in range(freqs):
         shift = shift_ref[w]
-        value = jnp.zeros((nbr, share), F32)
-        for d in range(1, reach + 1):
+        value = summed[(reach - 1) * nbr :]
+        for d in range(1, reach):
             value = jnp.where(shift == d, summed[(d - 1) * nbr : d * nbr], value)
         pol_ref[w] = value
 
@@ -664,7 +664,7 @@
             pltpu.VMEM((2, packed * fold, LANES), F32),
             pltpu.VMEM((2 * reach, nbr, atoms), F32),
             pltpu.VMEM((2, 2 * reach, 8, atoms), F32),
-            dma((3,)), *[pltpu.SemaphoreType.REGULAR] * 3,
+            dma((2,)), *[pltpu.SemaphoreType.REGULAR] * 3,
             dma((1,)), dma((2,)), dma((1,)), dma((parts,)), dma((parts,)), dma((1,)), dma((1,)),
         ],
         compiler_params=pltpu.CompilerParams(

time: 14.5 us -> 14.4 us (level)
  no operation moved by 1% of the time
where the time goes in v6:
time: 14.4 us; the launch traced here: 14.2 us
  Pallas kernels  13.5 us (94%)
  between operations  0.64 us (4%)
    pallas_call x1, Pallas kernels, body(): pl.pallas_call(functools.partial(kernel, reach), out_shape=(jax.ShapeDtyp...  12.8 us
    pallas_call x1, Pallas kernels, body(): pl.pallas_call(finish, out_shape=(jax.ShapeDtypeStruct((order, order, ato...  0.71 us

profile of v6, /device:TPU:0, one launch (start us, length us, event | category | flops | bytes accessed | tf_op | source)
XLA Modules:
  0.0 14.2 jit_solution(12708524241216727786)
XLA Ops:
  0.6 12.8 %shard_map.68 = (bf16[12,12,384]{2,1,0:T(8,128)(2,1)S(1)}, f32[48,4,48]{2,1,0:T(4,128)S(1)}) custom-call(s32[48]{0:T(128)} %shift_hbm.1, bf16[12,12,384]{2,1,0:T(8,128)(2,1)} %bitcast.6, bf16[144,4,384]{2,1,0:T(4,128)(2,1)} %bitcast.5, f32[96,4,384]{2,1,0:T(4,128)} %bitcast.4, s32[4,384]{1,0:T(4,128)} %near_hbm.1), custom_call_target="tpu_custom_call" | custom-call | tf_op jit(solution)/shard_map/pallas_call | solution.py:627
  13.5 0.7 %shard_map.69 = (bf16[12,12,384]{2,1,0:T(8,128)(2,1)}, f32[48,4,48]{2,1,0:T(4,128)}) custom-call(bf16[12,12,384]{2,1,0:T(8,128)(2,1)S(1)} %get-tuple-element.6.cor_ref, f32[48,4,48]{2,1,0:T(4,128)S(1)} %get-tuple-element.7.pol_ref), custom_call_target="tpu_custom_call" | custom-call | tf_op jit(solution)/shard_map/pallas_call | solution.py:685

commit v7 on v6

--- a/solution.py
+++ b/solution.py
@@ -497,41 +497,50 @@
         for r in range(1, ne):
             chunk_copy(r).start()
 
+    def hand_out(n):
+        start, stop, _, _ = plan[n]
+        for t in range(tiles):
+            lanes = slice(t * LANES, (t + 1) * LANES)
+            for s in range(2 * reach):
+                pout[s, start:stop, lanes] = side_partials(late, t, s, start, stop).astype(BF16)
+
+        @pl.when(even)
+        def _():
+            for e, slot in straight[0]:
+
+                @pl.when(reaches(me + e))
+                def _():
+                    part_copy(outgoing(e), pin.at[slot], start, stop, e).start()
+
+            for number, (e, _) in enumerate(shared):
+
+                @pl.when(reaches(me + e))
+                def _():
+                    share_copy(outgoing(e), number, start, stop).start()
+
+            part_copy(outgoing(1), pin.at[0], start, stop, 1).start()
+
+        @pl.when(odd)
+        def _():
+            for e, slot in straight[1]:
+
+                @pl.when(reaches(me + e))
+                def _():
+                    part_copy(outgoing(e), pin.at[slot], start, stop, e).start()
+
+            part_copy(outgoing(-1), pin.at[0], start, stop, -1).start()
+
     for n, (start, stop, first, final) in enumerate(plan):
         if first < final:
             side_products(late, first, final)
             if final == order:
                 pl.when(me >= ne // 2)(correlations)
-        for t in range(tiles):
-            lanes = slice(t * LANES, (t + 1) * LANES)
-            for s in range(2 * reach):
-                pout[s, start:stop, lanes] = side_partials(late, t, s, start, stop).astype(BF16)
-
-        @pl.when(even)
-        def _():
-            for e, slot in straight[0]:
-
-                @pl.when(reaches(me + e))
-                def _():
-                    part_copy(outgoing(e), pin.at[slot], start, stop, e).start()
-
-            for number, (e, _) in enumerate(shared):
-
-                @pl.when(reaches(me + e))
-                def _():
-                    share_copy(outgoing(e), number, start, stop).start()
-
-            part_copy(outgoing(1), pin.at[0], start, stop, 1).start()
-
-        @pl.when(odd)
-        def _():
-            for e, slot in straight[1]:
-
-                @pl.when(reaches(me + e))
-                def _():
-                    part_copy(outgoing(e), pin.at[slot], start, stop, e).start()
-
-            part_copy(outgoing(-1), pin.at[0], start, stop, -1).start()
+        if final < order and n == 0:
+            pl.when(me < ne // 2)(functools.partial(hand_out, n))
+        else:
+            if n == 1:
+                pl.when(me >= ne // 2)(functools.partial(hand_out, 0))
+            hand_out(n)
 
     pl.when(me < ne // 2)(correlations)
 

time: 14.4 us -> 14.4 us (level)
  no operation moved by 1% of the time
where the time goes in v7:
time: 14.4 us; the launch traced here: 14.2 us
  Pallas kernels  13.5 us (94%)
  between operations  0.64 us (4%)
    pallas_call x1, Pallas kernels, body(): pl.pallas_call(functools.partial(kernel, reach), out_shape=(jax.ShapeDtyp...  12.8 us
    pallas_call x1, Pallas kernels, body(): pl.pallas_call(finish, out_shape=(jax.ShapeDtypeStruct((order, order, ato...  0.71 us

profile of v7, /device:TPU:0, one launch (start us, length us, event | category | flops | bytes accessed | tf_op | source)
XLA Modules:
  0.0 14.2 jit_solution(2373737874915653771)
XLA Ops:
  0.6 12.8 %shard_map.68 = (bf16[12,12,384]{2,1,0:T(8,128)(2,1)S(1)}, f32[48,4,48]{2,1,0:T(4,128)S(1)}) custom-call(s32[48]{0:T(128)} %shift_hbm.1, bf16[12,12,384]{2,1,0:T(8,128)(2,1)} %bitcast.6, bf16[144,4,384]{2,1,0:T(4,128)(2,1)} %bitcast.5, f32[96,4,384]{2,1,0:T(4,128)} %bitcast.4, s32[4,384]{1,0:T(4,128)} %near_hbm.1), custom_call_target="tpu_custom_call" | custom-call | tf_op jit(solution)/shard_map/pallas_call | solution.py:636
  13.5 0.7 %shard_map.69 = (bf16[12,12,384]{2,1,0:T(8,128)(2,1)}, f32[48,4,48]{2,1,0:T(4,128)}) custom-call(bf16[12,12,384]{2,1,0:T(8,128)(2,1)S(1)} %get-tuple-element.6.cor_ref, f32[48,4,48]{2,1,0:T(4,128)S(1)} %get-tuple-element.7.pol_ref), custom_call_target="tpu_custom_call" | custom-call | tf_op jit(solution)/shard_map/pallas_call | solution.py:694
